TPU v7x, 32 devices: a whole 2x2x4 slice. The times are simulated.
32 devices in a mesh: clip: 1, head: 16 (over z, y, x), kv: 2 (over core).
Axes of the slice: x: 2, y: 2, z: 4, core: 2. Of those that a mesh axis runs over, the one named last changes fastest.
Arguments:
- queries: bfloat16 [4096, 4096], P(('clip', 'head')), may hold values from -7 to 7
- keys: bfloat16 [8192, 4096], P(('clip', 'head', 'kv')), may hold values from -5 to 5
- values: bfloat16 [8192, 4096], P(('clip', 'head', 'kv')), may hold values from -6 to 6
- tile_list: int32 [32, 32], P('clip'), may hold values from 0 to 63, as said below
Outputs:
- attended: bfloat16 [4096, 4096], P(('clip', 'head', 'kv'))
Inputs may be any that keep to these rules, and one draw needn't show every extreme that they name: `tile_list`: each row names 32 different key tiles. Calling a tile t even when (t // 2) is even, a row names at most 20 even tiles and at most 20 others; some row names exactly 20 even tiles and some row exactly 20 others, in every draw.
All inputs are finite; a program needn't handle non-finite values.
Results may differ from a plain program's by a relative error of at most 0.014.
Values may be sent and summed in bfloat16 or wider, within the bound.
No kernel may reach another device: no remote copies, remote signals or barrier semaphores. Data moves between devices by JAX's collectives and lax.ppermute only.
A program may use at most 128 MiB of HBM per device.

v0:
```python
import math

import jax
import jax.numpy as jnp
from jax import lax
from jax.sharding import PartitionSpec as P

HEADS = 32
DH = 128
TILE = 128
KTOK_DEV = 256


def local(queries, keys, values, tile_list):
    n_head = lax.axis_size("head")
    heads_dev = HEADS // n_head
    kv_index = lax.axis_index("kv")
    key_all, value_all = (
        lax.all_to_all(keys, "head", split_axis=1, concat_axis=0, tiled=True),
        lax.all_to_all(values, "head", split_axis=1, concat_axis=0, tiled=True),
    )
    tile_span = KTOK_DEV // TILE
    key_shard = tile_list // tile_span
    parity = key_shard % 2
    local_tile = key_shard // 2 * tile_span + tile_list % tile_span
    inv_root = 1.0 / jnp.sqrt(jnp.float32(DH))
    feat_width = key_all.shape[1]
    half_rows = queries.shape[0] // 2
    own_rows = lax.dynamic_slice_in_dim(queries, kv_index * half_rows, half_rows, 0)
    query_part = lax.all_to_all(own_rows, "head", split_axis=1, concat_axis=0, tiled=True)
    key_source, value_source = (
        lax.all_gather(key_all, "kv", axis=0, tiled=True),
        lax.all_gather(value_all, "kv", axis=0, tiled=True),
    )
    full_tile = parity * (key_all.shape[0] // TILE) + local_tile
    unit_rows = min(half_rows, TILE)
    unit_count = query_part.shape[0] // unit_rows
    unit_pos = jnp.arange(unit_count, dtype=jnp.int32) * unit_rows
    source_head = unit_pos // half_rows
    first_row = source_head * (2 * half_rows) + kv_index * half_rows + unit_pos % half_rows
    unit_tile = first_row // TILE
    query_tile_ids = jnp.arange(tile_list.shape[0], dtype=jnp.int32)
    onehot = (unit_tile[:, None] == query_tile_ids[None, :]).astype(jnp.int32)
    unit_lists = jnp.sum(onehot[:, :, None] * full_tile[None, :, :], axis=1)
    block_units = math.gcd(unit_count, max(1, 512 // unit_rows))
    key_tiles = key_source.reshape(-1, TILE, feat_width)
    value_tiles = value_source.reshape(-1, TILE, feat_width)
    slot_count = unit_lists.shape[1]

    def unit_block(block_index):
        query_block = lax.dynamic_slice_in_dim(
            query_part, block_index * block_units * unit_rows, block_units * unit_rows, 0
        )
        query_block = query_block.reshape(block_units, unit_rows, heads_dev, DH)
        tile_ids = lax.dynamic_slice_in_dim(unit_lists, block_index * block_units, block_units, 0)
        key_block = key_tiles[tile_ids].reshape(block_units, slot_count * TILE, heads_dev, DH)
        value_block = value_tiles[tile_ids].reshape(block_units, slot_count * TILE, heads_dev, DH)
        scores = (
            jnp.einsum(
                "bqhd,bkhd->bhqk", query_block, key_block, preferred_element_type=jnp.float32
            )
            * inv_root
        )
        row_peak = jnp.max(scores, axis=-1)
        exponent = jnp.exp(scores - row_peak[..., None])
        row_total = jnp.sum(exponent, axis=-1)
        weight = exponent.astype(jnp.bfloat16)
        weighted = jnp.einsum(
            "bhqk,bkhd->bqhd", weight, value_block, preferred_element_type=jnp.float32
        )
        result = weighted / jnp.transpose(row_total, (0, 2, 1))[..., None]
        return result.astype(jnp.bfloat16).reshape(block_units * unit_rows, feat_width)

    block_rows = lax.map(unit_block, jnp.arange(unit_count // block_units, dtype=jnp.int32))
    normalized = block_rows.reshape(n_head, -1, feat_width)
    regrouped = lax.all_to_all(normalized, "head", split_axis=0, concat_axis=2, tiled=True)
    return regrouped.reshape(-1, HEADS * DH)


def solution(mesh):
    return jax.shard_map(
        local,
        mesh=mesh,
        in_specs=(
            P(("clip", "head"), None),
            P(("clip", "head", "kv"), None),
            P(("clip", "head", "kv"), None),
            P("clip", None),
        ),
        out_specs=P(("clip", "head", "kv"), None),
        check_vma=False,
    )
```

profile of v0, /device:TPU:0, one launch (start us, length us, event | category | flops | bytes accessed | tf_op | source)
XLA Modules:
  0.0 509.9 jit_solution(12329036469467087044)
XLA Ops:
  14.6 57.2 %all_to_all.72 = bf16[256,16,256]{2,0,1:T(8,128)(2,1)} all-to-all(bf16[256,16,256]{2,0,1:T(8,128)(2,1)} %copy.50), channel_id=1, replica_groups=mesh['clip'=1,'head'=16,'kv'=2] {'head'}, dimensions={1} | all-to-all | bytes 4194304 | tf_op jit(solution)/shard_map/all_to_all | solution.py:20
  80.2 52.0 %all_to_all.73 = bf16[256,16,256]{2,0,1:T(8,128)(2,1)} all-to-all(bf16[256,16,256]{2,0,1:T(8,128)(2,1)} %copy.54), channel_id=1, replica_groups=mesh['clip'=1,'head'=16,'kv'=2] {'head'}, dimensions={1} | all-to-all | bytes 4194304 | tf_op jit(solution)/shard_map/all_to_all | solution.py:19
  137.9 22.8 %all-to-all-done.1 = bf16[128,16,256]{0,2,1:T(8,128)(2,1)S(1)} async-done(((bf16[128,16,256]{0,2,1:T(8,128)(2,1)}), bf16[128,16,256]{0,2,1:T(8,128)(2,1)S(1)}, u32[]{:S(2)}, u32[]{:S(2)}) %all-to-all-start.1) | async-done | bytes 1048608 | tf_op jit(solution)/shard_map/all_to_all | solution.py:30
  161.3 307.3 %while.12 = (s32[]{:T(128)}, bf16[4,512,256]{2,1,0:T(8,128)(2,1)}, s32[4]{0:T(128)S(1)}, s32[16,32]{1,0:T(8,128)S(1)}, bf16[64,128,256]{2,1,0:T(8,128)(2,1)}, /*...) while((s32[]{:T(128)}, bf16[4,512,256]{2,1,0:T(8,128)(2,1)}, ...), condition=%wide.region_4.5_spmd, body=%wide.region_1.4_spmd.sunk | while | flops 2181299712 | bytes 137391856 | solution.py:74
  171.6 12.6 %reshape.157 = bf16[4,4096,2,128]{3,2,1,0:T(2,128)(2,1)} reshape(bf16[128,128,256]{2,1,0:T(8,128)(2,1)} %gather_fusion) | data formatting | bytes 16777216 | tf_op jit(solution)/shard_map/while/body/eval_jaxpr/reshape | solution.py:56
  185.0 11.5 %multiply_reduce_fusion.3 = (f32[4,2,128]{2,1,0:T(2,128)S(1)}, f32[4,2,128,4096]{3,2,1,0:T(8,128)}) fusion(bf16[4,4096,2,128]{3,2,1,0:T(2,128)(2,1)} %reshape.157, bf16[4,128,2,128]{3,2,1,0:T(2,128)(2,1)S(1)} %reshape.158), kind=kOutput, calls=%fused_computation.3.clone.1 | convolution fusion | flops 1082129408 | bytes 25432064 | tf_op jit(solution)/shard_map/while/body/eval_jaxpr/bqhd,bkhd->bhqk/dot_general | solution.py:59
  205.2 12.6 %reshape.159 = bf16[4,4096,2,128]{3,2,1,0:T(2,128)(2,1)} reshape(bf16[128,128,256]{2,1,0:T(8,128)(2,1)} %gather_fusion.1) | data formatting | bytes 16777216 | tf_op jit(solution)/shard_map/while/body/eval_jaxpr/reshape | solution.py:57
  226.4 10.8 %fusion.45 = bf16[4,128,2,128]{1,3,2,0:T(8,128)(2,1)S(1)} fusion(f32[4,2,128,4096]{3,2,1,0:T(8,128)} %get-tuple-element.156, f32[4,2,128]{2,1,0:T(2,128)S(1)} %get-tuple-element.157, bf16[4,4096,2,128]{3,2,1,0:T(2,128)(2,1)} %reshape.159, f32[4,128,2]{1,2,0:T(2,128)S(1)} %bitcast.45), kind=kOutput, calls=%fused_computation.14.clone.1 | convolution fusion | flops 1086586880 | bytes 25436160 | tf_op jit(solution)/shard_map/while/body/eval_jaxpr/bhqk,bkhd->bqhd/dot_general | solution.py:68
  239.6 8.8 %gather_fusion = bf16[128,128,256]{2,1,0:T(8,128)(2,1)} fusion(bf16[64,128,256]{2,1,0:T(8,128)(2,1)} %get-tuple-element.190, s32[1024]{0:T(1024)S(1)} %pad_clamp_fusion.2), kind=kCustom, calls=%fused_computation.1.clone.1 | custom fusion | bytes 16777728 | tf_op jit(solution)/shard_map/while/body/eval_jaxpr/gather | solution.py:56
  248.4 12.6 %reshape.157 = bf16[4,4096,2,128]{3,2,1,0:T(2,128)(2,1)} reshape(bf16[128,128,256]{2,1,0:T(8,128)(2,1)} %gather_fusion) | data formatting | bytes 16777216 | tf_op jit(solution)/shard_map/while/body/eval_jaxpr/reshape | solution.py:56
  261.7 11.5 %multiply_reduce_fusion.3 = (f32[4,2,128]{2,1,0:T(2,128)S(1)}, f32[4,2,128,4096]{3,2,1,0:T(8,128)}) fusion(bf16[4,4096,2,128]{3,2,1,0:T(2,128)(2,1)} %reshape.157, bf16[4,128,2,128]{3,2,1,0:T(2,128)(2,1)S(1)} %reshape.158), kind=kOutput, calls=%fused_computation.3.clone.1 | convolution fusion | flops 1082129408 | bytes 25432064 | tf_op jit(solution)/shard_map/while/body/eval_jaxpr/bqhd,bkhd->bhqk/dot_general | solution.py:59
  281.9 12.6 %reshape.159 = bf16[4,4096,2,128]{3,2,1,0:T(2,128)(2,1)} reshape(bf16[128,128,256]{2,1,0:T(8,128)(2,1)} %gather_fusion.1) | data formatting | bytes 16777216 | tf_op jit(solution)/shard_map/while/body/eval_jaxpr/reshape | solution.py:57
  303.1 10.8 %fusion.45 = bf16[4,128,2,128]{1,3,2,0:T(8,128)(2,1)S(1)} fusion(f32[4,2,128,4096]{3,2,1,0:T(8,128)} %get-tuple-element.156, f32[4,2,128]{2,1,0:T(2,128)S(1)} %get-tuple-element.157, bf16[4,4096,2,128]{3,2,1,0:T(2,128)(2,1)} %reshape.159, f32[4,128,2]{1,2,0:T(2,128)S(1)} %bitcast.45), kind=kOutput, calls=%fused_computation.14.clone.1 | convolution fusion | flops 1086586880 | bytes 25436160 | tf_op jit(solution)/shard_map/while/body/eval_jaxpr/bhqk,bkhd->bqhd/dot_general | solution.py:68
  316.4 8.7 %gather_fusion = bf16[128,128,256]{2,1,0:T(8,128)(2,1)} fusion(bf16[64,128,256]{2,1,0:T(8,128)(2,1)} %get-tuple-element.190, s32[1024]{0:T(1024)S(1)} %pad_clamp_fusion.2), kind=kCustom, calls=%fused_computation.1.clone.1 | custom fusion | bytes 16777728 | tf_op jit(solution)/shard_map/while/body/eval_jaxpr/gather | solution.py:56
  325.2 12.6 %reshape.157 = bf16[4,4096,2,128]{3,2,1,0:T(2,128)(2,1)} reshape(bf16[128,128,256]{2,1,0:T(8,128)(2,1)} %gather_fusion) | data formatting | bytes 16777216 | tf_op jit(solution)/shard_map/while/body/eval_jaxpr/reshape | solution.py:56
  338.5 11.5 %multiply_reduce_fusion.3 = (f32[4,2,128]{2,1,0:T(2,128)S(1)}, f32[4,2,128,4096]{3,2,1,0:T(8,128)}) fusion(bf16[4,4096,2,128]{3,2,1,0:T(2,128)(2,1)} %reshape.157, bf16[4,128,2,128]{3,2,1,0:T(2,128)(2,1)S(1)} %reshape.158), kind=kOutput, calls=%fused_computation.3.clone.1 | convolution fusion | flops 1082129408 | bytes 25432064 | tf_op jit(solution)/shard_map/while/body/eval_jaxpr/bqhd,bkhd->bhqk/dot_general | solution.py:59
  358.7 12.6 %reshape.159 = bf16[4,4096,2,128]{3,2,1,0:T(2,128)(2,1)} reshape(bf16[128,128,256]{2,1,0:T(8,128)(2,1)} %gather_fusion.1) | data formatting | bytes 16777216 | tf_op jit(solution)/shard_map/while/body/eval_jaxpr/reshape | solution.py:57
  379.9 10.8 %fusion.45 = bf16[4,128,2,128]{1,3,2,0:T(8,128)(2,1)S(1)} fusion(f32[4,2,128,4096]{3,2,1,0:T(8,128)} %get-tuple-element.156, f32[4,2,128]{2,1,0:T(2,128)S(1)} %get-tuple-element.157, bf16[4,4096,2,128]{3,2,1,0:T(2,128)(2,1)} %reshape.159, f32[4,128,2]{1,2,0:T(2,128)S(1)} %bitcast.45), kind=kOutput, calls=%fused_computation.14.clone.1 | convolution fusion | flops 1086586880 | bytes 25436160 | tf_op jit(solution)/shard_map/while/body/eval_jaxpr/bhqk,bkhd->bqhd/dot_general | solution.py:68
  393.2 8.8 %gather_fusion = bf16[128,128,256]{2,1,0:T(8,128)(2,1)} fusion(bf16[64,128,256]{2,1,0:T(8,128)(2,1)} %get-tuple-element.190, s32[1024]{0:T(1024)S(1)} %pad_clamp_fusion.2), kind=kCustom, calls=%fused_computation.1.clone.1 | custom fusion | bytes 16777728 | tf_op jit(solution)/shard_map/while/body/eval_jaxpr/gather | solution.py:56
  401.9 12.6 %reshape.157 = bf16[4,4096,2,128]{3,2,1,0:T(2,128)(2,1)} reshape(bf16[128,128,256]{2,1,0:T(8,128)(2,1)} %gather_fusion) | data formatting | bytes 16777216 | tf_op jit(solution)/shard_map/while/body/eval_jaxpr/reshape | solution.py:56
  415.3 11.5 %multiply_reduce_fusion.3 = (f32[4,2,128]{2,1,0:T(2,128)S(1)}, f32[4,2,128,4096]{3,2,1,0:T(8,128)}) fusion(bf16[4,4096,2,128]{3,2,1,0:T(2,128)(2,1)} %reshape.157, bf16[4,128,2,128]{3,2,1,0:T(2,128)(2,1)S(1)} %reshape.158), kind=kOutput, calls=%fused_computation.3.clone.1 | convolution fusion | flops 1082129408 | bytes 25432064 | tf_op jit(solution)/shard_map/while/body/eval_jaxpr/bqhd,bkhd->bhqk/dot_general | solution.py:59
  435.5 12.6 %reshape.159 = bf16[4,4096,2,128]{3,2,1,0:T(2,128)(2,1)} reshape(bf16[128,128,256]{2,1,0:T(8,128)(2,1)} %gather_fusion.1) | data formatting | bytes 16777216 | tf_op jit(solution)/shard_map/while/body/eval_jaxpr/reshape | solution.py:57
  456.7 10.8 %fusion.45 = bf16[4,128,2,128]{1,3,2,0:T(8,128)(2,1)S(1)} fusion(f32[4,2,128,4096]{3,2,1,0:T(8,128)} %get-tuple-element.156, f32[4,2,128]{2,1,0:T(2,128)S(1)} %get-tuple-element.157, bf16[4,4096,2,128]{3,2,1,0:T(2,128)(2,1)} %reshape.159, f32[4,128,2]{1,2,0:T(2,128)S(1)} %bitcast.45), kind=kOutput, calls=%fused_computation.14.clone.1 | convolution fusion | flops 1086586880 | bytes 25436160 | tf_op jit(solution)/shard_map/while/body/eval_jaxpr/bhqk,bkhd->bqhd/dot_general | solution.py:68
  468.5 31.0 %all_to_all.74 = bf16[16,128,256]{2,1,0:T(8,128)(2,1)S(1)} all-to-all(bf16[16,128,256]{2,1,0:T(8,128)(2,1)} %bitcast.15), channel_id=1, replica_groups=mesh['clip'=1,'head'=16,'kv'=2] {'head'}, dimensions={0} | all-to-all | bytes 2097152 | tf_op jit(solution)/shard_map/all_to_all | solution.py:76
  (73 shorter events, 111.9 us)
Async XLA Ops:
  6.5 125.7 %copy-start = (bf16[256,4096]{1,0:T(8,128)(2,1)S(1)}, bf16[256,4096]{1,0:T(8,128)(2,1)}, u32[]{:S(2)}) copy-start(bf16[256,4096]{1,0:T(8,128)(2,1)} %param.6) | copy-start | bytes 6291460
  6.5 154.7 %all-gather.3.cloned.1.call-start = ((), (), s32[]{:S(2)}) async-start(), calls=%async_computation.4 | async-start | bytes 6291456 | tf_op jit(solution)/shard_map/all_gather | solution.py:33
  71.9 89.3 %all-gather.5.cloned.1.call-start = ((), (), s32[]{:S(2)}) async-start(), calls=%async_computation.5 | async-start | bytes 6291456 | tf_op jit(solution)/shard_map/all_gather | solution.py:32
  76.0 61.6 %copy-start.2 = (s32[32,32]{1,0:T(8,128)S(1)}, s32[32,32]{1,0:T(8,128)}, u32[]{:S(2)}) copy-start(s32[32,32]{1,0:T(8,128)} %param.9) | copy-start | bytes 12292
  133.6 27.1 %all-to-all-start.1 = ((bf16[128,16,256]{0,2,1:T(8,128)(2,1)}), bf16[128,16,256]{0,2,1:T(8,128)(2,1)S(1)}, u32[]{:S(2)}, u32[]{:S(2)}) async-start(bf16[128,16,256]{0,2,1:T(8,128)(2,1)} %bitcast.8), calls=%async_computation.1 | async-start | bytes 2097152 | tf_op jit(solution)/shard_map/all_to_all | solution.py:30
  468.5 34.6 %copy-start.1 = (bf16[256,4096]{1,0:T(8,128)(2,1)S(1)}, bf16[256,4096]{1,0:T(8,128)(2,1)}, u32[]{:S(2)}) copy-start(bf16[256,4096]{1,0:T(8,128)(2,1)} %param.6) | copy-start | bytes 6291460
Sparse Core Ops, SparseCore 0:
  72.0 11.9 all-gather.2
  132.3 11.9 all-gather.4
where the time goes:
time: 514 us; the launch traced here: 510 us
  local copies, waits for them, and re-layouts  200 us (39%)
  blocking collectives  140 us (27%)
  matrix products  88.9 us (17%)
  other arithmetic  34.8 us (7%)
  waiting for transfers between devices  22.9 us (4%)
  between operations  13.5 us (3%)
  loops' own time  5.86 us (1%)
    all_to_all x1, blocking collectives, local(): lax.all_to_all(values, 'head', split_axis=1, concat_axis=0, tiled=True)  57.2 us
    all_to_all x1, blocking collectives, local(): lax.all_to_all(keys, 'head', split_axis=1, concat_axis=0, tiled=True)  52 us
    reshape x4, local copies, waits for them, and re-layouts, unit_block(): key_tiles[tile_ids].reshape(block_units, slot_count * TILE, heads_dev, DH)  50.3 us
    reshape x4, local copies, waits for them, and re-layouts, unit_block(): value_tiles[tile_ids].reshape(block_units, slot_count * TILE, heads_dev, DH)  50.3 us
    dot_general x4, matrix products, unit_block(): jnp.einsum('bqhd,bkhd->bhqk', query_block, key_block, preferred_element_t...  45.9 us
    dot_general x4, matrix products, unit_block(): jnp.einsum('bhqk,bkhd->bqhd', weight, value_block, preferred_element_type...  43 us
    gather x4, local copies, waits for them, and re-layouts, unit_block(): key_tiles[tile_ids].reshape(block_units, slot_count * TILE, heads_dev, DH)  35 us
    gather x4, local copies, waits for them, and re-layouts, unit_block(): value_tiles[tile_ids].reshape(block_units, slot_count * TILE, heads_dev, DH)  34.9 us
  transfers between devices with their start and end apart: 3, of which 1 were waited for; matrix products, arithmetic and copies ran while one was open for 2% of the time, Pallas kernels for 0%

commit v1 on v0

v1 whole, which is shorter than its diff:
```python
import functools
import math

import jax
import jax.numpy as jnp
from jax import lax
from jax.experimental import pallas as pl
from jax.experimental.pallas import tpu as pltpu
from jax.sharding import PartitionSpec as P

HEADS = 32
DH = 128
TILE = 128
CHUNK = 4
GROUPS = 2
LOW = -1e30


def block_kernel(q_ref, k_ref, v_ref, qo_ref, ko_ref, vo_ref):
    qo_ref[0] = q_ref[...]
    ko_ref[0] = k_ref[...]
    vo_ref[0] = v_ref[...]


def split_columns(kv_index, queries, keys, values, parts):
    half_rows = queries.shape[0] // 2
    width = queries.shape[1] // parts
    k_rows = keys.shape[0]
    grid_spec = pltpu.PrefetchScalarGridSpec(
        num_scalar_prefetch=1,
        grid=(parts,),
        in_specs=[
            pl.BlockSpec((half_rows, width), lambda j, c: (c[0], j)),
            pl.BlockSpec((k_rows, width), lambda j, c: (0, j)),
            pl.BlockSpec((k_rows, width), lambda j, c: (0, j)),
        ],
        out_specs=[
            pl.BlockSpec((1, half_rows, width), lambda j, c: (j, 0, 0)),
            pl.BlockSpec((1, k_rows, width), lambda j, c: (j, 0, 0)),
            pl.BlockSpec((1, k_rows, width), lambda j, c: (j, 0, 0)),
        ],
    )

    def body(c_ref, *refs):
        block_kernel(*refs)

    return pl.pallas_call(
        body,
        grid_spec=grid_spec,
        out_shape=[
            jax.ShapeDtypeStruct((parts, half_rows, width), queries.dtype),
            jax.ShapeDtypeStruct((parts, k_rows, width), keys.dtype),
            jax.ShapeDtypeStruct((parts, k_rows, width), values.dtype),
        ],
        name="split_columns",
    )(kv_index.reshape(1), queries, keys, values)


def attend_kernel(
    heads, tiles_src, lists_ref, counts_ref, q_ref, k0, k1, v0, v1, o_ref, st_ref,
    k_scr, v_scr, m_scr, l_scr, acc_scr, sems,
):
    unit = pl.program_id(0)

    @pl.when(unit == 0)
    def _():
        copies = [
            pltpu.make_async_copy(src, dst.at[pl.ds(base, tiles_src)], sems.at[n])
            for n, (src, dst, base) in enumerate(
                ((k0, k_scr, 0), (k1, k_scr, tiles_src), (v0, v_scr, 0), (v1, v_scr, tiles_src))
            )
        ]
        for copy in copies:
            copy.start()
        for copy in copies:
            copy.wait()

    scale = math.log2(math.e) / math.sqrt(DH)
    count = counts_ref[unit]
    m_scr[...] = jnp.full_like(m_scr, LOW)
    l_scr[...] = jnp.zeros_like(l_scr)
    acc_scr[...] = jnp.zeros_like(acc_scr)

    def step(first, masked):
        ids = [lists_ref[unit, first + n] for n in range(CHUNK)]
        for h in range(heads):
            cols = pl.ds(h * DH, DH)
            k_block = jnp.concatenate([k_scr[t, :, cols] for t in ids], axis=0)
            v_block = jnp.concatenate([v_scr[t, :, cols] for t in ids], axis=0)
            scores = lax.dot_general(
                q_ref[0, :, cols], k_block, (((1,), (1,)), ((), ())), preferred_element_type=jnp.float32
            )
            if masked:
                slot = first + lax.broadcasted_iota(jnp.int32, (1, CHUNK * TILE), 1) // TILE
                scores = jnp.where(slot < count, scores, LOW)
            m_old = m_scr[h]
            peak = jnp.max(scores, axis=1, keepdims=True)
            m_new = jnp.maximum(m_old, peak)
            m_scr[h] = m_new
            expo = jnp.exp2((scores - m_new[:, :1]) * scale)
            if masked:
                expo = jnp.where(slot < count, expo, 0.0)
            alpha = jnp.exp2((m_old - m_new) * scale)
            part = expo[:, :TILE]
            for n in range(1, CHUNK):
                part = part + expo[:, n * TILE : (n + 1) * TILE]
            l_scr[h] = l_scr[h] * alpha + part
            acc_scr[h] = acc_scr[h] * alpha + jnp.dot(
                expo.astype(jnp.bfloat16), v_block, preferred_element_type=jnp.float32
            )

    full = count // CHUNK

    def loop_body(i, carry):
        step(i * CHUNK, False)
        return carry

    lax.fori_loop(0, full, loop_body, 0)

    @pl.when(count % CHUNK != 0)
    def _():
        step(full * CHUNK, True)

    lane = lax.broadcasted_iota(jnp.int32, (TILE, TILE), 1)
    stats = jnp.full((TILE, TILE), LOW, jnp.float32)
    for h in range(heads):
        total = jnp.sum(l_scr[h], axis=1, keepdims=True)
        some = total > 0.0
        safe = jnp.where(some, total, 1.0)
        o_ref[0, :, pl.ds(h * DH, DH)] = (acc_scr[h] / safe).astype(o_ref.dtype)
        level = jnp.where(some, m_scr[h][:, :1] * scale + jnp.log2(safe), LOW)
        stats = jnp.where(lane == h, level, stats)
    st_ref[0] = stats.T[: st_ref.shape[1]]


def attend(lists, counts, q, k_pair, v_pair):
    units, rows, width = q.shape
    heads = width // DH
    stat_rows = -(-heads // 8) * 8
    as_tiles = lambda t: t.reshape(-1, TILE, width)
    k_pair = [as_tiles(t) for t in k_pair]
    v_pair = [as_tiles(t) for t in v_pair]
    tiles_src = k_pair[0].shape[0]
    anywhere = pl.BlockSpec(memory_space=pl.ANY)
    grid_spec = pltpu.PrefetchScalarGridSpec(
        num_scalar_prefetch=2,
        grid=(units,),
        in_specs=[pl.BlockSpec((1, rows, width), lambda u, *_: (u, 0, 0))] + [anywhere] * 4,
        out_specs=[
            pl.BlockSpec((1, rows, width), lambda u, *_: (u, 0, 0)),
            pl.BlockSpec((1, stat_rows, TILE), lambda u, *_: (u, 0, 0)),
        ],
        scratch_shapes=[
            pltpu.VMEM((2 * tiles_src, TILE, width), jnp.bfloat16),
            pltpu.VMEM((2 * tiles_src, TILE, width), jnp.bfloat16),
            pltpu.VMEM((heads, TILE, TILE), jnp.float32),
            pltpu.VMEM((heads, TILE, TILE), jnp.float32),
            pltpu.VMEM((heads, TILE, DH), jnp.float32),
            pltpu.SemaphoreType.DMA((4,)),
        ],
    )
    return pl.pallas_call(
        functools.partial(attend_kernel, heads, tiles_src),
        grid_spec=grid_spec,
        out_shape=[
            jax.ShapeDtypeStruct((units, rows, width), jnp.bfloat16),
            jax.ShapeDtypeStruct((units, stat_rows, TILE), jnp.float32),
        ],
        name="attend",
    )(lists, counts, q, *k_pair, *v_pair)


def merge_kernel(heads, oa_ref, sa_ref, ob_ref, sb_ref, o_ref):
    pad = jnp.zeros((TILE - sa_ref.shape[1], TILE), jnp.float32)
    level_a = jnp.concatenate([sa_ref[0], pad], axis=0).T
    level_b = jnp.concatenate([sb_ref[0], pad], axis=0).T
    top = jnp.maximum(level_a, level_b)
    weight_a = jnp.exp2(level_a - top)
    weight_b = jnp.exp2(level_b - top)
    total = weight_a + weight_b
    weight_a = weight_a / total
    weight_b = weight_b / total
    for h in range(heads):
        cols = pl.ds(h * DH, DH)
        merged = oa_ref[0, :, cols].astype(jnp.float32) * weight_a[:, h : h + 1]
        merged = merged + ob_ref[0, :, cols].astype(jnp.float32) * weight_b[:, h : h + 1]
        o_ref[0, :, cols] = merged.astype(o_ref.dtype)


def merge(oa, sa, ob, sb):
    units, rows, width = oa.shape
    stat_rows = sa.shape[1]
    o_spec = pl.BlockSpec((1, rows, width), lambda u: (u, 0, 0))
    s_spec = pl.BlockSpec((1, stat_rows, TILE), lambda u: (u, 0, 0))
    return pl.pallas_call(
        functools.partial(merge_kernel, width // DH),
        grid=(units,),
        in_specs=[o_spec, s_spec, o_spec, s_spec],
        out_specs=o_spec,
        out_shape=jax.ShapeDtypeStruct(oa.shape, oa.dtype),
        name="merge",
    )(oa, sa, ob, sb)


def join_kernel(x_ref, o_ref):
    o_ref[...] = x_ref[0]


def join_columns(x):
    parts, rows, width = x.shape
    return pl.pallas_call(
        join_kernel,
        grid=(parts,),
        in_specs=[pl.BlockSpec((1, rows, width), lambda j: (j, 0, 0))],
        out_specs=pl.BlockSpec((rows, width), lambda j: (0, j)),
        out_shape=jax.ShapeDtypeStruct((rows, parts * width), x.dtype),
        name="join_columns",
    )(x)


def key_lists(tile_list, span, group, kv_index, members):
    shard = tile_list // span
    owner = shard // 2
    inside = owner // members == group
    local = jnp.where(shard % 2 == kv_index, 0, members * span) + owner % members * span + tile_list % span
    slots = tile_list.shape[1]
    slot = jnp.arange(slots, dtype=jnp.int32)
    before = (slot[:, None] < slot[None, :]).astype(jnp.int32)
    flag = inside.astype(jnp.int32)
    place = jnp.sum(flag[:, :, None] * before[None], axis=1)
    hit = inside[:, :, None] & (place[:, :, None] == slot[None, None, :])
    packed = jnp.sum(jnp.where(hit, local[:, :, None], 0), axis=1)
    return packed, jnp.sum(flag, axis=1)


def local(queries, keys, values, tile_list):
    n_head = lax.axis_size("head")
    members = n_head // GROUPS
    kv_index = lax.axis_index("kv")
    head_index = lax.axis_index("head")
    group = head_index // members
    groups = [list(range(g * members, (g + 1) * members)) for g in range(GROUPS)]
    across = [(i, (i + members) % n_head) for i in range(n_head)]
    swap = [(0, 1), (1, 0)]

    exchange = functools.partial(
        lax.all_to_all, axis_name="head", split_axis=0, concat_axis=0, axis_index_groups=groups, tiled=True
    )
    q_blocks, k_blocks, v_blocks = split_columns(kv_index, queries, keys, values, members)
    q_own = exchange(q_blocks)
    q_far = lax.ppermute(q_own, "head", across)
    k_own = exchange(k_blocks)
    k_other = lax.ppermute(k_own, "kv", swap)
    v_own = exchange(v_blocks)
    v_other = lax.ppermute(v_own, "kv", swap)

    packed, number = key_lists(tile_list, keys.shape[0] // TILE, group, kv_index, members)
    units_src = queries.shape[0] // 2 // TILE
    packed = packed.reshape(GROUPS, members, 2, units_src, -1)
    number = number.reshape(GROUPS, members, 2, units_src)

    def lists_of(g):
        pick = lambda t: lax.dynamic_index_in_dim(
            lax.dynamic_index_in_dim(t, g, 0, False), kv_index, 1, False
        )
        return pick(packed).reshape(members * units_src, -1), pick(number).reshape(-1)

    width = q_own.shape[2]
    as_units = lambda t: t.reshape(members * units_src, TILE, width)
    lists, counts = lists_of(1 - group)
    o_far, s_far = attend(lists, counts, as_units(q_far), (k_own, k_other), (v_own, v_other))
    o_back = lax.ppermute(o_far, "head", across)
    s_back = lax.ppermute(s_far, "head", across)
    lists, counts = lists_of(group)
    o_near, s_near = attend(lists, counts, as_units(q_own), (k_own, k_other), (v_own, v_other))
    merged = merge(o_near, s_near, o_back, s_back).reshape(members, -1, width)
    return join_columns(exchange(merged))


def solution(mesh):
    return jax.shard_map(
        local,
        mesh=mesh,
        in_specs=(
            P(("clip", "head"), None),
            P(("clip", "head", "kv"), None),
            P(("clip", "head", "kv"), None),
            P("clip", None),
        ),
        out_specs=P(("clip", "head", "kv"), None),
        check_vma=False,
    )
```

time: 514 us -> 288 us (0.56)
  local copies, waits for them, and re-layouts: 200 us -> 2.46 us
  Pallas kernels: 0 us -> 144 us
  matrix products: 88.9 us -> 0 us
  blocking collectives: 140 us -> 78.1 us
  other arithmetic: 34.8 us -> 0.96 us
  waiting for transfers between devices: 22.9 us -> 51.8 us
  between operations: 13.5 us -> 0.14 us
  loops' own time: 5.86 us -> 0 us
    pallas_call x0 -> x5, Pallas kernels: none -> 144 us  [the longest x2 125 us: attend(): pl.pallas_call(functools.partial(attend_kernel, heads, tiles_src), grid_s...]
    reshape x13 -> x1, local copies, waits for them, and re-layouts: 103 us -> 0.08 us  [local(): number = number.reshape(GROUPS, members, 2, units_src)]
    dot_general x8 -> x0, matrix products: 88.9 us -> none  [the longest x4 45.9 us: unit_block(): jnp.einsum('bqhd,bkhd->bhqk', query_block, key_block, preferred_element_t...]
    gather x8 -> x0, local copies, waits for them, and re-layouts: 69.9 us -> none  [the longest x4 35 us: unit_block(): key_tiles[tile_ids].reshape(block_units, slot_count * TILE, heads_dev, DH)]
    all_to_all x3, blocking collectives: 140 us -> 78.1 us  [the longest x1 32.6 us: local(): k_own = exchange(k_blocks)]
    ppermute x0 -> x5, waiting for transfers between devices: none -> 39 us  [the longest x1 38.9 us: local(): q_far = lax.ppermute(q_own, 'head', across)]
    reduce_sum x5 -> x3, other arithmetic: 34.6 us -> 0.95 us  [the longest x1 0.57 us: key_lists(): packed = jnp.sum(jnp.where(hit, local[:, :, None], 0), axis=1)]
    all_to_all x1, waiting for transfers between devices: 22.8 us -> 12.8 us  [local(): q_own = exchange(q_blocks)]
  transfers between devices with their start and end apart: 3 -> 6, of which waited for: 1 -> 2; matrix products, arithmetic and copies ran while one was open for 2% -> 1% of each run, Pallas kernels for 0% -> 28%
where the time goes in v1:
time: 288 us; the launch traced here: 286 us
  Pallas kernels  144 us (50%)
  blocking collectives  78.1 us (27%)
  waiting for transfers between devices  51.8 us (18%)
  starting transfers between devices  8.34 us (3%)
    pallas_call x2, Pallas kernels, attend(): pl.pallas_call(functools.partial(attend_kernel, heads, tiles_src), grid_s...  125 us
    ppermute x1, waiting for transfers between devices, local(): q_far = lax.ppermute(q_own, 'head', across)  38.9 us
    all_to_all x1, blocking collectives, local(): k_own = exchange(k_blocks)  32.6 us
    all_to_all x1, blocking collectives, local(): v_own = exchange(v_blocks)  28.2 us
    all_to_all x1, blocking collectives, local(): return join_columns(exchange(merged))  17.2 us
    all_to_all x1, waiting for transfers between devices, local(): q_own = exchange(q_blocks)  12.8 us
    pallas_call x1, Pallas kernels, split_columns(): pl.pallas_call(body, grid_spec=grid_spec, out_shape=[jax.ShapeDtypeStruct...  7.16 us
    pallas_call x1, Pallas kernels, merge(): pl.pallas_call(functools.partial(merge_kernel, width // DH), grid=(units,...  7.03 us
  transfers between devices with their start and end apart: 6, of which 2 were waited for; matrix products, arithmetic and copies ran while one was open for 1% of the time, Pallas kernels for 28%

profile of v1, /device:TPU:0, one launch (start us, length us, event | category | flops | bytes accessed | tf_op | source)
XLA Modules:
  0.0 285.7 jit_solution(13594802507827391023)
XLA Ops:
  0.0 7.2 %split_columns.1 = (bf16[8,128,512]{2,1,0:T(8,128)(2,1)}, bf16[8,256,512]{2,1,0:T(8,128)(2,1)}, bf16[8,256,512]{2,1,0:T(8,128)(2,1)}) custom-call(s32[1]{0:T(128)} %bitcast.2.c_ref, bf16[256,4096]{1,0:T(8,128)(2,1)} %refs_0_.1, bf16[256,4096]{1,0:T(8,128)(2,1)} %refs_1_.1, bf16[256,4096]{1,0:T(8,128)(2,1)} %refs_2_.1), custom_call_target="tpu_custom_call" | custom-call | tf_op jit(solution)/shard_map/split_columns/pallas_call | solution.py:47
  7.2 32.6 %all_to_all.20 = bf16[8,256,512]{2,1,0:T(8,128)(2,1)S(1)} all-to-all(bf16[8,256,512]{2,1,0:T(8,128)(2,1)} %get-tuple-element.13), channel_id=1, replica_groups={{0,2,4,6,8,10,12,14},{16,18,20,22,24,26,28,30},{1,3,5,7,9,11,13,15},{17..., dimensions={0} | all-to-all | bytes 4194304 | tf_op jit(solution)/shard_map/all_to_all | solution.py:252
  39.8 28.2 %all_to_all.21 = bf16[8,256,512]{2,1,0:T(8,128)(2,1)} all-to-all(bf16[8,256,512]{2,1,0:T(8,128)(2,1)S(1)} %copy-done.2), channel_id=1, replica_groups={{0,2,4,6,8,10,12,14},{16,18,20,22,24,26,28,30},{1,3,5,7,9,11,13,15},{17..., dimensions={0} | all-to-all | bytes 4194304 | tf_op jit(solution)/shard_map/all_to_all | solution.py:254
  68.0 3.7 %all-to-all-start = ((bf16[8,128,512]{2,1,0:T(8,128)(2,1)}), bf16[8,128,512]{2,1,0:T(8,128)(2,1)S(1)}, u32[]{:S(2)}, u32[]{:S(2)}) async-start(bf16[8,128,512]{2,1,0:T(8,128)(2,1)} %get-tuple-element.12), calls=%async_computation | async-start | bytes 2097152 | tf_op jit(solution)/shard_map/all_to_all | solution.py:250
  71.7 0.1 collective-permute-start
  71.8 0.5 collective-permute-start.1
  72.3 12.8 %all-to-all-done.q_ref = bf16[8,128,512]{2,1,0:T(8,128)(2,1)S(1)} async-done(((bf16[8,128,512]{2,1,0:T(8,128)(2,1)}), bf16[8,128,512]{2,1,0:T(8,128)(2,1)S(1)}, u32[]{:S(2)}, u32[]{:S(2)}) %all-to-all-start) | async-done | bytes 1048608 | tf_op jit(solution)/shard_map/all_to_all | solution.py:250
  85.1 1.1 collective-permute-start.2
  86.2 0.2 convert_reduce_fusion
  86.4 0.1 reshape.68
  86.5 0.8 dynamic-slice_reduce_fusion
  87.3 0.2 multiply_reduce_fusion
  87.5 0.6 select_reduce_fusion
  88.1 0.6 constant_dynamic-slice_fusion
  88.7 38.9 %collective-permute-done.2.q_ref = bf16[8,128,512]{2,1,0:T(8,128)(2,1)} collective-permute-done((bf16[8,128,512]{2,1,0:T(8,128)(2,1)S(1)}, bf16[8,128,512]{2,1,0:T(8,128)(2,1)}, u32[]{:S(2)}, u32[]{:S(2)}) %collective-permute-start.2) | collective-permute-done | bytes 1048608 | tf_op jit(solution)/shard_map/ppermute | solution.py:251
  127.6 44.1 %attend.3 = (bf16[8,128,512]{2,1,0:T(8,128)(2,1)}, f32[8,8,128]{2,1,0:T(8,128)}) custom-call(s32[8,32]{1,0:T(8,128)} %bitcast.14, s32[8]{0:T(128)} %get-tuple-element.19.counts_ref, bf16[8,128,512]{2,1,0:T(8,128)(2,1)} %collective-permute-done.2.q_ref, bf16[16,128,512]{2,1,0:T(8,128)(2,1)} %bitcast.8, bf16[16,128,512]{2,1,0:T(8,128)(2,1)} %bitcast.4.k1, ...), custom_call_target="tpu_custom_call" | custom-call | tf_op jit(solution)/shard_map/attend/pallas_call | solution.py:162
  171.8 0.1 collective-permute-start.3
  171.9 2.9 %collective-permute-start.4 = (f32[8,8,128]{2,1,0:T(8,128)}, f32[8,8,128]{2,1,0:T(8,128)S(1)}, u32[]{:S(2)}, u32[]{:S(2)}) collective-permute-start(f32[8,8,128]{2,1,0:T(8,128)} %get-tuple-element.18), channel_id=1, source_target_pairs={{0,16},{2,18},{4,20},{6,22},{8,24},{10,26},{12,28},{14,30},{16,0},... | collective-permute-start | bytes 98312 | tf_op jit(solution)/shard_map/ppermute | solution.py:273
  174.8 80.5 %attend.2 = (bf16[8,128,512]{2,1,0:T(8,128)(2,1)}, f32[8,8,128]{2,1,0:T(8,128)}) custom-call(s32[8,32]{1,0:T(8,128)} %bitcast.13, s32[8]{0:T(128)} %get-tuple-element.20.counts_ref, bf16[8,128,512]{2,1,0:T(8,128)(2,1)} %copy-done.1, bf16[16,128,512]{2,1,0:T(8,128)(2,1)} %bitcast.9, bf16[16,128,512]{2,1,0:T(8,128)(2,1)} %bitcast.4.k1, ...), custom_call_target="tpu_custom_call" | custom-call | tf_op jit(solution)/shard_map/attend/pallas_call | solution.py:162
  255.4 0.6 copy-done.4
  255.9 0.4 copy-done.3
  256.3 7.0 %merge.1 = bf16[8,128,512]{2,1,0:T(8,128)(2,1)} custom-call(bf16[8,128,512]{2,1,0:T(8,128)(2,1)} %get-tuple-element.15.oa_ref, f32[8,8,128]{2,1,0:T(8,128)} %get-tuple-element.16.sa_ref, bf16[8,128,512]{2,1,0:T(8,128)(2,1)} %copy-done.3, f32[8,8,128]{2,1,0:T(8,128)} %copy-done.4), custom_call_target="tpu_custom_call" | custom-call | tf_op jit(solution)/shard_map/merge/pallas_call | solution.py:195
  263.4 17.2 %all_to_all.22.x_ref = bf16[8,128,512]{2,1,0:T(8,128)(2,1)} all-to-all(bf16[8,128,512]{2,1,0:T(8,128)(2,1)} %merge.1), channel_id=1, replica_groups={{0,2,4,6,8,10,12,14},{16,18,20,22,24,26,28,30},{1,3,5,7,9,11,13,15},{17..., dimensions={0} | all-to-all | bytes 2097152 | tf_op jit(solution)/shard_map/all_to_all | solution.py:277
  280.6 5.2 %join_columns.1 = bf16[128,4096]{1,0:T(8,128)(2,1)} custom-call(bf16[8,128,512]{2,1,0:T(8,128)(2,1)} %all_to_all.22.x_ref), custom_call_target="tpu_custom_call" | custom-call | tf_op jit(solution)/shard_map/join_columns/pallas_call | solution.py:211
  (16 shorter events, 0.0 us)
Async XLA Ops:
  7.2 32.6 %copy-start.2 = (bf16[8,256,512]{2,1,0:T(8,128)(2,1)S(1)}, bf16[8,256,512]{2,1,0:T(8,128)(2,1)}, u32[]{:S(2)}) copy-start(bf16[8,256,512]{2,1,0:T(8,128)(2,1)} %get-tuple-element.14) | copy-start | bytes 6291460
  39.8 31.9 %copy-start = (bf16[8,256,512]{2,1,0:T(8,128)(2,1)}, bf16[8,256,512]{2,1,0:T(8,128)(2,1)S(1)}, u32[]{:S(2)}) copy-start(bf16[8,256,512]{2,1,0:T(8,128)(2,1)S(1)} %all_to_all.20) | copy-start | bytes 6291460
  68.0 18.2 %copy-start.5 = (s32[32,32]{1,0:T(8,128)S(1)}, s32[32,32]{1,0:T(8,128)}, u32[]{:S(2)}) copy-start(s32[32,32]{1,0:T(8,128)} %param.7) | copy-start | bytes 12292
  68.0 17.1 %all-to-all-start = ((bf16[8,128,512]{2,1,0:T(8,128)(2,1)}), bf16[8,128,512]{2,1,0:T(8,128)(2,1)S(1)}, u32[]{:S(2)}, u32[]{:S(2)}) async-start(bf16[8,128,512]{2,1,0:T(8,128)(2,1)} %get-tuple-element.12), calls=%async_computation | async-start | bytes 2097152 | tf_op jit(solution)/shard_map/all_to_all | solution.py:250
  71.7 55.9 %collective-permute-start = (bf16[8,256,512]{2,1,0:T(8,128)(2,1)S(1)}, bf16[8,256,512]{2,1,0:T(8,128)(2,1)}, u32[]{:S(2)}, u32[]{:S(2)}) collective-permute-start(bf16[8,256,512]{2,1,0:T(8,128)(2,1)S(1)} %all_to_all.20), channel_id=1, source_target_pairs={{0,1},{1,0},{2,3},{3,2},{4,5},{5,4},{6,7},{7,6},{8,9},{9,8},{10,11... | collective-permute-start | bytes 6291464 | tf_op jit(solution)/shard_map/ppermute | solution.py:253
  71.8 55.8 %collective-permute-start.1 = (bf16[8,256,512]{2,1,0:T(8,128)(2,1)}, bf16[8,256,512]{2,1,0:T(8,128)(2,1)}, u32[]{:S(2)}, u32[]{:S(2)}) collective-permute-start(bf16[8,256,512]{2,1,0:T(8,128)(2,1)} %all_to_all.21), channel_id=1, source_target_pairs={{0,1},{1,0},{2,3},{3,2},{4,5},{5,4},{6,7},{7,6},{8,9},{9,8},{10,11... | collective-permute-start | bytes 6291464 | tf_op jit(solution)/shard_map/ppermute | solution.py:255
  85.1 86.7 %copy-start.1 = (bf16[8,128,512]{2,1,0:T(8,128)(2,1)}, bf16[8,128,512]{2,1,0:T(8,128)(2,1)S(1)}, u32[]{:S(2)}) copy-start(bf16[8,128,512]{2,1,0:T(8,128)(2,1)S(1)} %all-to-all-done.q_ref) | copy-start | bytes 3145732
  85.1 42.5 %collective-permute-start.2 = (bf16[8,128,512]{2,1,0:T(8,128)(2,1)S(1)}, bf16[8,128,512]{2,1,0:T(8,128)(2,1)}, u32[]{:S(2)}, u32[]{:S(2)}) collective-permute-start(bf16[8,128,512]{2,1,0:T(8,128)(2,1)S(1)} %all-to-all-done.q_ref), channel_id=1, source_target_pairs={{0,16},{2,18},{4,20},{6,22},{8,24},{10,26},{12,28},{14,30},{16,0},... | collective-permute-start | bytes 3145736 | tf_op jit(solution)/shard_map/ppermute | solution.py:251
  171.8 83.6 %collective-permute-start.3 = (bf16[8,128,512]{2,1,0:T(8,128)(2,1)}, bf16[8,128,512]{2,1,0:T(8,128)(2,1)S(1)}, u32[]{:S(2)}, u32[]{:S(2)}) collective-permute-start(bf16[8,128,512]{2,1,0:T(8,128)(2,1)} %get-tuple-element.17), channel_id=1, source_target_pairs={{0,16},{2,18},{4,20},{6,22},{8,24},{10,26},{12,28},{14,30},{16,0},... | collective-permute-start | bytes 3145736 | tf_op jit(solution)/shard_map/ppermute | solution.py:272
  171.9 83.5 %collective-permute-start.4 = (f32[8,8,128]{2,1,0:T(8,128)}, f32[8,8,128]{2,1,0:T(8,128)S(1)}, u32[]{:S(2)}, u32[]{:S(2)}) collective-permute-start(f32[8,8,128]{2,1,0:T(8,128)} %get-tuple-element.18), channel_id=1, source_target_pairs={{0,16},{2,18},{4,20},{6,22},{8,24},{10,26},{12,28},{14,30},{16,0},... | collective-permute-start | bytes 98312 | tf_op jit(solution)/shard_map/ppermute | solution.py:273
  255.3 0.6 copy-start.4
  255.4 1.0 copy-start.3

commit v2 on v1

v2 whole, which is shorter than its diff:
```python
import functools
import math

import jax
import jax.numpy as jnp
from jax import lax
from jax.experimental import pallas as pl
from jax.experimental.pallas import tpu as pltpu
from jax.sharding import PartitionSpec as P


HEADS = 32
DH = 128
TILE = 128
STEP = 8
GROUPS = 2
LOW = -1e30
SCALE = math.log2(math.e) / math.sqrt(DH)


def split_queries(kv_index, queries, members, parts):
    rows = queries.shape[0] // 2
    width = queries.shape[1] // (members * parts)

    def body(c_ref, q_ref, *rest):
        outs, sems = rest[:parts], rest[parts]
        first = pl.multiple_of(c_ref[0] * rows, rows)
        copies = [
            pltpu.make_async_copy(
                q_ref.at[pl.ds(first, rows), pl.ds((j * parts + p) * width, width)], outs[p].at[j], sems.at[p, j]
            )
            for p in range(parts)
            for j in range(members)
        ]
        for copy in copies:
            copy.start()
        for copy in copies:
            copy.wait()

    anywhere = pl.BlockSpec(memory_space=pl.ANY)
    return pl.pallas_call(
        body,
        grid_spec=pltpu.PrefetchScalarGridSpec(
            num_scalar_prefetch=1,
            grid=(),
            in_specs=[anywhere],
            out_specs=[anywhere] * parts,
            scratch_shapes=[pltpu.SemaphoreType.DMA((parts, members))],
        ),
        out_shape=[jax.ShapeDtypeStruct((members, rows, width), queries.dtype)] * parts,
        name="split_queries",
    )(kv_index.reshape(1), queries)


def split_keys(keys, values, members, parts):
    rows, features = keys.shape
    tiles = rows // TILE
    heads = features // DH // (members * parts)
    group = math.gcd(members, 2)
    width = features // members * group

    def body(k_ref, v_ref, *outs):
        for g in range(group):
            for p in range(parts):
                for h in range(heads):
                    cols = pl.ds(((g * parts + p) * heads + h) * DH, DH)
                    for t in range(tiles):
                        outs[p][g, t, h] = k_ref[pl.ds(t * TILE, TILE), cols]
                        outs[p][g, t, heads + h] = v_ref[pl.ds(t * TILE, TILE), cols].T

    block = pl.BlockSpec((rows, width), lambda j: (0, j))
    return pl.pallas_call(
        body,
        grid=(members // group,),
        in_specs=[block, block],
        out_specs=[pl.BlockSpec((group, tiles, 2 * heads, TILE, DH), lambda j: (j, 0, 0, 0, 0))] * parts,
        out_shape=[jax.ShapeDtypeStruct((members, tiles, 2 * heads, TILE, DH), keys.dtype)] * parts,
        name="split_keys",
    )(keys, values)


def attend_kernel(
    heads, tiles_src, lists_ref, counts_ref, q_ref, near_ref, far_ref, o_ref, st_ref,
    kv_scr, m_scr, l_scr, acc_scr, sems,
):
    unit = pl.program_id(0)

    @pl.when(unit == 0)
    def _():
        copies = [
            pltpu.make_async_copy(src, kv_scr.at[pl.ds(n * tiles_src, tiles_src)], sems.at[n])
            for n, src in enumerate((near_ref, far_ref))
        ]
        for copy in copies:
            copy.start()
        for copy in copies:
            copy.wait()

    count = counts_ref[unit]
    m_scr[...] = jnp.full_like(m_scr, LOW)
    l_scr[...] = jnp.zeros_like(l_scr)
    acc_scr[...] = jnp.zeros_like(acc_scr)

    def step(first, size, masked):
        ids = [lists_ref[unit, first + n] for n in range(size)]
        scores = []
        for h in range(heads):
            k_block = jnp.concatenate([kv_scr[t, h] for t in ids], axis=0)
            scores.append(
                lax.dot_general(
                    k_block, q_ref[0, :, pl.ds(h * DH, DH)], (((1,), (1,)), ((), ())),
                    preferred_element_type=jnp.float32,
                )
            )
        if masked:
            slot = first + lax.broadcasted_iota(jnp.int32, (size * TILE, 1), 0) // TILE
            valid = slot < count
        for h in range(heads):
            score = jnp.where(valid, scores[h], LOW) if masked else scores[h]
            m_old = m_scr[h]
            peak = jnp.max(jnp.max(score.reshape(-1, 8, TILE), axis=0), axis=0, keepdims=True)
            m_new = jnp.maximum(m_old, peak)
            m_scr[h] = m_new
            expo = jnp.exp2((score - m_new[:1]) * SCALE)
            if masked:
                expo = jnp.where(valid, expo, 0.0)
            alpha = jnp.exp2((m_old - m_new) * SCALE)
            l_scr[h] = l_scr[h] * alpha + jnp.sum(expo.reshape(-1, 8, TILE), axis=0)
            v_block = jnp.concatenate([kv_scr[t, heads + h] for t in ids], axis=1)
            acc_scr[h] = acc_scr[h] * alpha[:1] + jnp.dot(
                v_block, expo.astype(jnp.bfloat16), preferred_element_type=jnp.float32
            )

    full = count // STEP
    rest = count - full * STEP

    def loop_body(i, carry):
        step(i * STEP, STEP, False)
        return carry

    lax.fori_loop(0, full, loop_body, 0)

    @pl.when(rest > STEP // 2)
    def _():
        step(full * STEP, STEP, True)

    @pl.when((rest > 0) & (rest <= STEP // 2))
    def _():
        step(full * STEP, STEP // 2, True)

    for h in range(heads):
        total = jnp.sum(l_scr[h], axis=0, keepdims=True)
        some = total > 0.0
        safe = jnp.where(some, total, 1.0)
        o_ref[0, :, pl.ds(h * DH, DH)] = (acc_scr[h] * (1.0 / safe)).astype(o_ref.dtype).T
        st_ref[0, h : h + 1] = jnp.where(some, m_scr[h][:1] * SCALE + jnp.log2(safe), LOW)


def attend(lists, counts, q, kv_near, kv_far):
    units, rows, width = q.shape
    heads = width // DH
    as_tiles = lambda t: t.reshape(-1, 2 * heads, TILE, DH)
    kv_near, kv_far = as_tiles(kv_near), as_tiles(kv_far)
    tiles_src = kv_near.shape[0]
    anywhere = pl.BlockSpec(memory_space=pl.ANY)
    grid_spec = pltpu.PrefetchScalarGridSpec(
        num_scalar_prefetch=2,
        grid=(units,),
        in_specs=[pl.BlockSpec((1, rows, width), lambda u, *_: (u, 0, 0))] + [anywhere] * 2,
        out_specs=[
            pl.BlockSpec((1, rows, width), lambda u, *_: (u, 0, 0)),
            pl.BlockSpec((1, 8, TILE), lambda u, *_: (u, 0, 0)),
        ],
        scratch_shapes=[
            pltpu.VMEM((2 * tiles_src, 2 * heads, TILE, DH), jnp.bfloat16),
            pltpu.VMEM((heads, 8, TILE), jnp.float32),
            pltpu.VMEM((heads, 8, TILE), jnp.float32),
            pltpu.VMEM((heads, DH, TILE), jnp.float32),
            pltpu.SemaphoreType.DMA((2,)),
        ],
    )
    return pl.pallas_call(
        functools.partial(attend_kernel, heads, tiles_src),
        grid_spec=grid_spec,
        out_shape=[
            jax.ShapeDtypeStruct((units, rows, width), jnp.bfloat16),
            jax.ShapeDtypeStruct((units, 8, TILE), jnp.float32),
        ],
        name="attend",
    )(lists, counts, q, kv_near, kv_far)


def merge_kernel(heads, units, oa_ref, sa_ref, ob_ref, sb_ref, o_ref):
    for u in range(units):
        top = jnp.maximum(sa_ref[u], sb_ref[u])
        weight_a = jnp.exp2(sa_ref[u] - top)
        weight_b = jnp.exp2(sb_ref[u] - top)
        total = weight_a + weight_b
        weights = jnp.concatenate([weight_a / total, weight_b / total], axis=0)
        weights = jnp.concatenate([weights, jnp.zeros((TILE - 16, TILE), jnp.float32)], axis=0).T
        for h in range(heads):
            cols = pl.ds(h * DH, DH)
            merged = oa_ref[u, :, cols].astype(jnp.float32) * weights[:, h : h + 1]
            merged = merged + ob_ref[u, :, cols].astype(jnp.float32) * weights[:, 8 + h : 9 + h]
            o_ref[u, :, cols] = merged.astype(o_ref.dtype)


def merge(oa, sa, ob, sb):
    units, rows, width = oa.shape
    some = math.gcd(units, 4)
    o_spec = pl.BlockSpec((some, rows, width), lambda u: (u, 0, 0))
    s_spec = pl.BlockSpec((some, 8, TILE), lambda u: (u, 0, 0))
    return pl.pallas_call(
        functools.partial(merge_kernel, width // DH, some),
        grid=(units // some,),
        in_specs=[o_spec, s_spec, o_spec, s_spec],
        out_specs=o_spec,
        out_shape=jax.ShapeDtypeStruct(oa.shape, oa.dtype),
        name="merge",
    )(oa, sa, ob, sb)


def join_columns(blocks):
    parts = len(blocks)
    members, rows, width = blocks[0].shape

    def body(*refs):
        ins, o_ref, sems = refs[:parts], refs[parts], refs[parts + 1]
        copies = [
            pltpu.make_async_copy(ins[p].at[j], o_ref.at[:, pl.ds((j * parts + p) * width, width)], sems.at[p, j])
            for p in range(parts)
            for j in range(members)
        ]
        for copy in copies:
            copy.start()
        for copy in copies:
            copy.wait()

    anywhere = pl.BlockSpec(memory_space=pl.ANY)
    return pl.pallas_call(
        body,
        in_specs=[anywhere] * parts,
        out_specs=anywhere,
        scratch_shapes=[pltpu.SemaphoreType.DMA((parts, members))],
        out_shape=jax.ShapeDtypeStruct((rows, members * parts * width), blocks[0].dtype),
        name="join_columns",
    )(*blocks)


def key_lists(tile_list, span, group, kv_index, members):
    shard = tile_list // span
    owner = shard // 2
    inside = owner // members == group
    local = jnp.where(shard % 2 == kv_index, 0, members * span) + owner % members * span + tile_list % span
    slots = tile_list.shape[1]
    slot = jnp.arange(slots, dtype=jnp.int32)
    before = (slot[:, None] < slot[None, :]).astype(jnp.int32)
    flag = inside.astype(jnp.int32)
    place = jnp.sum(flag[:, :, None] * before[None], axis=1)
    hit = inside[:, :, None] & (place[:, :, None] == slot[None, None, :])
    packed = jnp.sum(jnp.where(hit, local[:, :, None], 0), axis=1)
    return packed, jnp.sum(flag, axis=1)


def local(queries, keys, values, tile_list):
    n_head = lax.axis_size("head")
    members = n_head // GROUPS
    parts = math.gcd(HEADS // members, 2)
    kv_index = lax.axis_index("kv")
    head_index = lax.axis_index("head")
    group = head_index // members
    groups = [list(range(g * members, (g + 1) * members)) for g in range(GROUPS)]
    across = [(i, (i + members) % n_head) for i in range(n_head)]
    swap = [(0, 1), (1, 0)]
    units_src = queries.shape[0] // 2 // TILE
    units = members * units_src

    exchange = functools.partial(
        lax.all_to_all, axis_name="head", split_axis=0, concat_axis=0, axis_index_groups=groups, tiled=True
    )
    then = lambda first, later: lax.optimization_barrier((first, later))

    packed, number = key_lists(tile_list, keys.shape[0] // TILE, group, kv_index, members)
    packed = packed.reshape(GROUPS, members, 2, units_src, -1)
    number = number.reshape(GROUPS, members, 2, units_src)

    def lists_of(g):
        pick = lambda t: lax.dynamic_index_in_dim(
            lax.dynamic_index_in_dim(t, g, 0, False), kv_index, 1, False
        )
        return pick(packed).reshape(units, -1), pick(number).reshape(-1)

    far_lists, near_lists = lists_of(1 - group), lists_of(group)

    as_units = lambda t: t.reshape(units, TILE, t.shape[2])
    q_blocks = split_queries(kv_index, queries, members, parts)
    kv_blocks = list(split_keys(keys, values, members, parts))

    q_near, q_far, kv = [], [], []
    for p in range(parts):
        q_block, kv_block = q_blocks[p], kv_blocks[p]
        if p:
            kv[p - 1], q_block = then(kv[p - 1], q_block)
        q_got = exchange(q_block)
        q_got, kv_block = then(q_got, kv_block)
        q_near.append(as_units(q_got))
        q_far.append(as_units(lax.ppermute(q_got, "head", across)))
        kv.append(exchange(kv_block))

    blocks = []
    for p in range(parts):
        kv_other = lax.ppermute(kv[p], "kv", swap)
        o_far, s_far = attend(*far_lists, q_far[p], kv[p], kv_other)
        o_back = lax.ppermute(o_far, "head", across)
        s_back = lax.ppermute(s_far, "head", across)
        o_near, s_near = attend(*near_lists, q_near[p], kv[p], kv_other)
        merged = merge(o_near, s_near, o_back, s_back)
        blocks.append(exchange(merged.reshape(members, -1, merged.shape[2])))
    return join_columns(blocks)


def solution(mesh):
    return jax.shard_map(
        local,
        mesh=mesh,
        in_specs=(
            P(("clip", "head"), None),
            P(("clip", "head", "kv"), None),
            P(("clip", "head", "kv"), None),
            P("clip", None),
        ),
        out_specs=P(("clip", "head", "kv"), None),
        check_vma=False,
    )
```

time: 288 us -> 308 us (1.069)
  blocking collectives: 78.1 us -> 52.9 us
  waiting for transfers between devices: 51.8 us -> 73.1 us
  starting transfers between devices: 8.34 us -> 22.2 us
  Pallas kernels: 144 us -> 154 us
    pallas_call x3 -> x5, Pallas kernels: 19.3 us -> 76.7 us  [the longest x1 33 us: join_columns(): pl.pallas_call(body, in_specs=[anywhere] * parts, out_specs=anywhere, scr...]
    pallas_call x2 -> x4, Pallas kernels: 125 us -> 77.5 us  [attend(): pl.pallas_call(functools.partial(attend_kernel, heads, tiles_src), grid_s...]
    all_to_all x3, blocking collectives: 78.1 us -> 52.9 us  [the longest x1 29.4 us: local(): kv.append(exchange(kv_block))]
    ppermute x1 -> x2, waiting for transfers between devices: 0.01 us -> 24.3 us  [local(): s_back = lax.ppermute(s_far, 'head', across)]
    ppermute x3 -> x4, waiting for transfers between devices: 38.9 us -> 21.4 us  [the longest x2 21.4 us: local(): q_far.append(as_units(lax.ppermute(q_got, 'head', across)))]
    all_to_all x1 -> x3, waiting for transfers between devices: 12.8 us -> 27.3 us  [the longest x1 23.1 us: local(): kv.append(exchange(kv_block))]
    all_to_all x1 -> x3, starting transfers between devices: 3.69 us -> 13.4 us  [the longest x1 6.22 us: local(): q_got = exchange(q_block)]
    ppermute x3 -> x4, starting transfers between devices: 1.66 us -> 5.63 us  [the longest x2 5.56 us: local(): q_far.append(as_units(lax.ppermute(q_got, 'head', across)))]
  transfers between devices with their start and end apart: 6 -> 11, of which waited for: 2 -> 5; matrix products, arithmetic and copies ran while one was open for 1% -> 1% of each run, Pallas kernels for 28% -> 29%
where the time goes in v2:
time: 308 us; the launch traced here: 307 us
  Pallas kernels  154 us (50%)
  waiting for transfers between devices  73.1 us (24%)
  blocking collectives  52.9 us (17%)
  starting transfers between devices  22.2 us (7%)
  local copies, waits for them, and re-layouts  3.1 us (1%)
    pallas_call x4, Pallas kernels, attend(): pl.pallas_call(functools.partial(attend_kernel, heads, tiles_src), grid_s...  77.5 us
    pallas_call x1, Pallas kernels, join_columns(): pl.pallas_call(body, in_specs=[anywhere] * parts, out_specs=anywhere, scr...  33 us
    pallas_call x1, Pallas kernels, split_queries(): pl.pallas_call(body, grid_spec=pltpu.PrefetchScalarGridSpec(num_scalar_pr...  33 us
    all_to_all x1, blocking collectives, local(): kv.append(exchange(kv_block))  29.4 us
    ppermute x2, waiting for transfers between devices, local(): s_back = lax.ppermute(s_far, 'head', across)  24.3 us
    all_to_all x1, waiting for transfers between devices, local(): kv.append(exchange(kv_block))  23.1 us
    ppermute x2, waiting for transfers between devices, local(): q_far.append(as_units(lax.ppermute(q_got, 'head', across)))  21.4 us
    all_to_all x1, blocking collectives, local(): blocks.append(exchange(merged.reshape(members, -1, merged.shape[2])))  13.2 us
  transfers between devices with their start and end apart: 11, of which 5 were waited for; matrix products, arithmetic and copies ran while one was open for 1% of the time, Pallas kernels for 29%

profile of v2, /device:TPU:0, one launch (start us, length us, event | category | flops | bytes accessed | tf_op | source)
XLA Modules:
  0.0 306.7 jit_solution(13802453928254534007)
XLA Ops:
  0.0 33.0 %split_queries.1 = (bf16[8,128,256]{2,1,0:T(8,128)(2,1)}, bf16[8,128,256]{2,1,0:T(8,128)(2,1)}) custom-call(s32[1]{0:T(128)} %bitcast.2.c_ref, bf16[256,4096]{1,0:T(8,128)(2,1)} %q_ref.1), custom_call_target="tpu_custom_call" | custom-call | tf_op jit(solution)/shard_map/split_queries/pallas_call | solution.py:41
  33.0 6.2 %all-to-all-start = ((bf16[8,128,256]{2,1,0:T(8,128)(2,1)}), bf16[8,128,256]{2,1,0:T(8,128)(2,1)S(1)}, u32[]{:S(2)}, u32[]{:S(2)}) async-start(bf16[8,128,256]{2,1,0:T(8,128)(2,1)} %get-tuple-element.23), calls=%async_computation | async-start | bytes 1048576 | tf_op jit(solution)/shard_map/all_to_all | solution.py:304
  39.2 5.0 %split_keys.1 = (bf16[8,2,4,128,128]{4,3,2,1,0:T(8,128)(2,1)}, bf16[8,2,4,128,128]{4,3,2,1,0:T(8,128)(2,1)}) custom-call(bf16[256,4096]{1,0:T(8,128)(2,1)} %k_ref.1, bf16[256,4096]{1,0:T(8,128)(2,1)} %v_ref.1), custom_call_target="tpu_custom_call" | custom-call | tf_op jit(solution)/shard_map/split_keys/pallas_call | solution.py:72
  44.2 4.2 %all-to-all-done.q_ref = bf16[8,128,256]{2,1,0:T(8,128)(2,1)S(1)} async-done(((bf16[8,128,256]{2,1,0:T(8,128)(2,1)}), bf16[8,128,256]{2,1,0:T(8,128)(2,1)S(1)}, u32[]{:S(2)}, u32[]{:S(2)}) %all-to-all-start) | async-done | bytes 524320 | tf_op jit(solution)/shard_map/all_to_all | solution.py:304
  48.4 29.4 %all_to_all.30 = bf16[8,2,4,128,128]{4,3,2,1,0:T(8,128)(2,1)} all-to-all(bf16[8,2,4,128,128]{4,3,2,1,0:T(8,128)(2,1)} %get-tuple-element.26), channel_id=1, replica_groups={{0,2,4,6,8,10,12,14},{16,18,20,22,24,26,28,30},{1,3,5,7,9,11,13,15},{17..., dimensions={0} | all-to-all | bytes 4194304 | tf_op jit(solution)/shard_map/all_to_all | solution.py:308
  77.7 10.4 %all_to_all.31.q_ref = bf16[8,128,256]{2,1,0:T(8,128)(2,1)S(1)} all-to-all(bf16[8,128,256]{2,1,0:T(8,128)(2,1)S(1)} %copy-done.6), channel_id=1, replica_groups={{0,2,4,6,8,10,12,14},{16,18,20,22,24,26,28,30},{1,3,5,7,9,11,13,15},{17..., dimensions={0} | all-to-all | bytes 1048576 | tf_op jit(solution)/shard_map/all_to_all | solution.py:304
  88.1 3.7 %all-to-all-start.4 = ((bf16[8,2,4,128,128]{4,3,2,1,0:T(8,128)(2,1)}), bf16[8,2,4,128,128]{4,3,2,1,0:T(8,128)(2,1)S(1)}, u32[]{:S(2)}, u32[]{:S(2)}) async-start(bf16[8,2,4,128,128]{4,3,2,1,0:T(8,128)(2,1)} %get-tuple-element.36), calls=%async_computation.4 | async-start | bytes 4194304 | tf_op jit(solution)/shard_map/all_to_all | solution.py:308
  92.0 23.1 %all-to-all-done.4 = bf16[8,2,4,128,128]{4,3,2,1,0:T(8,128)(2,1)S(1)} async-done(((bf16[8,2,4,128,128]{4,3,2,1,0:T(8,128)(2,1)}), bf16[8,2,4,128,128]{4,3,2,1,0:T(8,128)(2,1)S(1)}, u32[]{:S(2)}, u32[]{:S(2)}) %all-to-all-start.4) | async-done | bytes 2097184 | tf_op jit(solution)/shard_map/all_to_all | solution.py:308
  115.1 2.7 collective-permute-start.1
  118.0 0.8 dynamic-slice_reduce_fusion
  120.3 21.4 %collective-permute-done.1.q_ref = bf16[8,128,256]{2,1,0:T(8,128)(2,1)} collective-permute-done((bf16[8,128,256]{2,1,0:T(8,128)(2,1)S(1)}, bf16[8,128,256]{2,1,0:T(8,128)(2,1)}, u32[]{:S(2)}, u32[]{:S(2)}) %collective-permute-start.1) | collective-permute-done | bytes 524320 | tf_op jit(solution)/shard_map/ppermute | solution.py:307
  141.7 15.5 %attend.5 = (bf16[8,128,256]{2,1,0:T(8,128)(2,1)}, f32[8,8,128]{2,1,0:T(8,128)}) custom-call(s32[8,32]{1,0:T(8,128)} %bitcast.15, s32[8]{0:T(128)} %get-tuple-element.41.counts_ref, bf16[8,128,256]{2,1,0:T(8,128)(2,1)} %collective-permute-done.1.q_ref, bf16[16,4,128,128]{3,2,1,0:T(8,128)(2,1)} %bitcast.10, bf16[16,4,128,128]{3,2,1,0:T(8,128)(2,1)} %bitcast.4.far_ref), custom_call_target="tpu_custom_call" | custom-call | tf_op jit(solution)/shard_map/attend/pallas_call | solution.py:182
  157.3 2.9 collective-permute-start.5
  160.3 23.3 %attend.4 = (bf16[8,128,256]{2,1,0:T(8,128)(2,1)}, f32[8,8,128]{2,1,0:T(8,128)}) custom-call(s32[8,32]{1,0:T(8,128)} %bitcast.13, s32[8]{0:T(128)} %get-tuple-element.42.counts_ref, bf16[8,128,256]{2,1,0:T(8,128)(2,1)} %copy-done.3, bf16[16,4,128,128]{3,2,1,0:T(8,128)(2,1)} %bitcast.11, bf16[16,4,128,128]{3,2,1,0:T(8,128)(2,1)} %bitcast.4.far_ref), custom_call_target="tpu_custom_call" | custom-call | tf_op jit(solution)/shard_map/attend/pallas_call | solution.py:182
  183.6 22.9 %collective-permute-done.3.sb_ref = f32[8,8,128]{2,1,0:T(8,128)S(1)} collective-permute-done((f32[8,8,128]{2,1,0:T(8,128)}, f32[8,8,128]{2,1,0:T(8,128)S(1)}, u32[]{:S(2)}, u32[]{:S(2)}) %collective-permute-start.3) | collective-permute-done | bytes 32800 | tf_op jit(solution)/shard_map/ppermute | solution.py:315
  207.3 2.9 merge.2
  210.2 3.5 %all-to-all-start.2 = ((bf16[8,128,256]{2,1,0:T(8,128)(2,1)}), bf16[8,128,256]{2,1,0:T(8,128)(2,1)S(1)}, u32[]{:S(2)}, u32[]{:S(2)}) async-start(bf16[8,128,256]{2,1,0:T(8,128)(2,1)} %merge.2), calls=%async_computation.2 | async-start | bytes 1048576 | tf_op jit(solution)/shard_map/all_to_all | solution.py:318
  213.7 15.5 %attend.7 = (bf16[8,128,256]{2,1,0:T(8,128)(2,1)}, f32[8,8,128]{2,1,0:T(8,128)}) custom-call(s32[8,32]{1,0:T(8,128)} %bitcast.16, s32[8]{0:T(128)} %get-tuple-element.41.counts_ref, bf16[8,128,256]{2,1,0:T(8,128)(2,1)} %collective-permute-done.5.q_ref, bf16[16,4,128,128]{3,2,1,0:T(8,128)(2,1)} %bitcast.8, bf16[16,4,128,128]{3,2,1,0:T(8,128)(2,1)} %bitcast.7.far_ref), custom_call_target="tpu_custom_call" | custom-call | tf_op jit(solution)/shard_map/attend/pallas_call | solution.py:182
  229.7 2.5 collective-permute-start.7
  232.2 23.2 %attend.6 = (bf16[8,128,256]{2,1,0:T(8,128)(2,1)}, f32[8,8,128]{2,1,0:T(8,128)}) custom-call(s32[8,32]{1,0:T(8,128)} %bitcast.14, s32[8]{0:T(128)} %get-tuple-element.42.counts_ref, bf16[8,128,256]{2,1,0:T(8,128)(2,1)} %copy-done.2, bf16[16,4,128,128]{3,2,1,0:T(8,128)(2,1)} %bitcast.9, bf16[16,4,128,128]{3,2,1,0:T(8,128)(2,1)} %bitcast.7.far_ref), custom_call_target="tpu_custom_call" | custom-call | tf_op jit(solution)/shard_map/attend/pallas_call | solution.py:182
  255.5 1.4 collective-permute-done.7.sb_ref
  257.7 2.9 merge.3
  260.5 13.2 %all_to_all.32.refs_1_ = bf16[8,128,256]{2,1,0:T(8,128)(2,1)} all-to-all(bf16[8,128,256]{2,1,0:T(8,128)(2,1)} %merge.3), channel_id=1, replica_groups={{0,2,4,6,8,10,12,14},{16,18,20,22,24,26,28,30},{1,3,5,7,9,11,13,15},{17..., dimensions={0} | all-to-all | bytes 1048576 | tf_op jit(solution)/shard_map/all_to_all | solution.py:318
  273.7 33.0 %join_columns.1 = bf16[128,4096]{1,0:T(8,128)(2,1)} custom-call(bf16[8,128,256]{2,1,0:T(8,128)(2,1)} %copy-done.1, bf16[8,128,256]{2,1,0:T(8,128)(2,1)} %all_to_all.32.refs_1_), custom_call_target="tpu_custom_call" | custom-call | tf_op jit(solution)/shard_map/join_columns/pallas_call | solution.py:240
  (38 shorter events, 4.0 us)
Async XLA Ops:
  33.0 15.3 %all-to-all-start = ((bf16[8,128,256]{2,1,0:T(8,128)(2,1)}), bf16[8,128,256]{2,1,0:T(8,128)(2,1)S(1)}, u32[]{:S(2)}, u32[]{:S(2)}) async-start(bf16[8,128,256]{2,1,0:T(8,128)(2,1)} %get-tuple-element.23), calls=%async_computation | async-start | bytes 1048576 | tf_op jit(solution)/shard_map/all_to_all | solution.py:304
  48.4 66.8 %copy-start.3 = (bf16[8,128,256]{2,1,0:T(8,128)(2,1)}, bf16[8,128,256]{2,1,0:T(8,128)(2,1)S(1)}, u32[]{:S(2)}) copy-start(bf16[8,128,256]{2,1,0:T(8,128)(2,1)S(1)} %all-to-all-done.q_ref) | copy-start | bytes 1572868
  48.4 29.4 %copy-start.6 = (bf16[8,128,256]{2,1,0:T(8,128)(2,1)S(1)}, bf16[8,128,256]{2,1,0:T(8,128)(2,1)}, u32[]{:S(2)}) copy-start(bf16[8,128,256]{2,1,0:T(8,128)(2,1)} %get-tuple-element.33) | copy-start | bytes 1572868
  88.1 69.1 %copy-start.2 = (bf16[8,128,256]{2,1,0:T(8,128)(2,1)}, bf16[8,128,256]{2,1,0:T(8,128)(2,1)S(1)}, u32[]{:S(2)}) copy-start(bf16[8,128,256]{2,1,0:T(8,128)(2,1)S(1)} %all_to_all.31.q_ref) | copy-start | bytes 1572868
  88.1 29.6 %copy-start.9 = (s32[32,32]{1,0:T(8,128)S(1)}, s32[32,32]{1,0:T(8,128)}, u32[]{:S(2)}) copy-start(s32[32,32]{1,0:T(8,128)} %param.7) | copy-start | bytes 12292
  88.1 27.0 %all-to-all-start.4 = ((bf16[8,2,4,128,128]{4,3,2,1,0:T(8,128)(2,1)}), bf16[8,2,4,128,128]{4,3,2,1,0:T(8,128)(2,1)S(1)}, u32[]{:S(2)}, u32[]{:S(2)}) async-start(bf16[8,2,4,128,128]{4,3,2,1,0:T(8,128)(2,1)} %get-tuple-element.36), calls=%async_computation.4 | async-start | bytes 4194304 | tf_op jit(solution)/shard_map/all_to_all | solution.py:308
  91.9 49.8 %collective-permute-start = (bf16[8,2,4,128,128]{4,3,2,1,0:T(8,128)(2,1)}, bf16[8,2,4,128,128]{4,3,2,1,0:T(8,128)(2,1)}, u32[]{:S(2)}, u32[]{:S(2)}) collective-permute-start(bf16[8,2,4,128,128]{4,3,2,1,0:T(8,128)(2,1)} %all_to_all.30), channel_id=1, source_target_pairs={{0,1},{1,0},{2,3},{3,2},{4,5},{5,4},{6,7},{7,6},{8,9},{9,8},{10,11... | collective-permute-start | bytes 6291464 | tf_op jit(solution)/shard_map/ppermute | solution.py:312
  115.1 42.1 %copy-start = (bf16[8,2,4,128,128]{4,3,2,1,0:T(8,128)(2,1)}, bf16[8,2,4,128,128]{4,3,2,1,0:T(8,128)(2,1)S(1)}, u32[]{:S(2)}) copy-start(bf16[8,2,4,128,128]{4,3,2,1,0:T(8,128)(2,1)S(1)} %all-to-all-done.4) | copy-start | bytes 6291460
  115.1 98.6 %collective-permute-start.4 = (bf16[8,2,4,128,128]{4,3,2,1,0:T(8,128)(2,1)S(1)}, bf16[8,2,4,128,128]{4,3,2,1,0:T(8,128)(2,1)}, u32[]{:S(2)}, u32[]{:S(2)}) collective-permute-start(bf16[8,2,4,128,128]{4,3,2,1,0:T(8,128)(2,1)S(1)} %all-to-all-done.4), channel_id=1, source_target_pairs={{0,1},{1,0},{2,3},{3,2},{4,5},{5,4},{6,7},{7,6},{8,9},{9,8},{10,11... | collective-permute-start | bytes 6291464 | tf_op jit(solution)/shard_map/ppermute | solution.py:312
  115.1 26.6 %collective-permute-start.1 = (bf16[8,128,256]{2,1,0:T(8,128)(2,1)S(1)}, bf16[8,128,256]{2,1,0:T(8,128)(2,1)}, u32[]{:S(2)}, u32[]{:S(2)}) collective-permute-start(bf16[8,128,256]{2,1,0:T(8,128)(2,1)S(1)} %all-to-all-done.q_ref), channel_id=1, source_target_pairs={{0,16},{2,18},{4,20},{6,22},{8,24},{10,26},{12,28},{14,30},{16,0},... | collective-permute-start | bytes 1572872 | tf_op jit(solution)/shard_map/ppermute | solution.py:307
  157.2 49.3 %collective-permute-start.2 = (bf16[8,128,256]{2,1,0:T(8,128)(2,1)}, bf16[8,128,256]{2,1,0:T(8,128)(2,1)S(1)}, u32[]{:S(2)}, u32[]{:S(2)}) collective-permute-start(bf16[8,128,256]{2,1,0:T(8,128)(2,1)} %get-tuple-element.31), channel_id=1, source_target_pairs={{0,16},{2,18},{4,20},{6,22},{8,24},{10,26},{12,28},{14,30},{16,0},... | collective-permute-start | bytes 1572872 | tf_op jit(solution)/shard_map/ppermute | solution.py:314
  157.3 56.4 %collective-permute-start.5 = (bf16[8,128,256]{2,1,0:T(8,128)(2,1)S(1)}, bf16[8,128,256]{2,1,0:T(8,128)(2,1)}, u32[]{:S(2)}, u32[]{:S(2)}) collective-permute-start(bf16[8,128,256]{2,1,0:T(8,128)(2,1)S(1)} %all_to_all.31.q_ref), channel_id=1, source_target_pairs={{0,16},{2,18},{4,20},{6,22},{8,24},{10,26},{12,28},{14,30},{16,0},... | collective-permute-start | bytes 1572872 | tf_op jit(solution)/shard_map/ppermute | solution.py:307
  160.2 46.3 %collective-permute-start.3 = (f32[8,8,128]{2,1,0:T(8,128)}, f32[8,8,128]{2,1,0:T(8,128)S(1)}, u32[]{:S(2)}, u32[]{:S(2)}) collective-permute-start(f32[8,8,128]{2,1,0:T(8,128)} %get-tuple-element.32), channel_id=1, source_target_pairs={{0,16},{2,18},{4,20},{6,22},{8,24},{10,26},{12,28},{14,30},{16,0},... | collective-permute-start | bytes 98312 | tf_op jit(solution)/shard_map/ppermute | solution.py:315
  206.5 0.6 copy-start.7
  206.5 0.8 copy-start.4
  210.2 50.4 %all-to-all-start.2 = ((bf16[8,128,256]{2,1,0:T(8,128)(2,1)}), bf16[8,128,256]{2,1,0:T(8,128)(2,1)S(1)}, u32[]{:S(2)}, u32[]{:S(2)}) async-start(bf16[8,128,256]{2,1,0:T(8,128)(2,1)} %merge.2), calls=%async_computation.2 | async-start | bytes 1048576 | tf_op jit(solution)/shard_map/all_to_all | solution.py:318
  229.2 27.7 %collective-permute-start.6 = (bf16[8,128,256]{2,1,0:T(8,128)(2,1)}, bf16[8,128,256]{2,1,0:T(8,128)(2,1)S(1)}, u32[]{:S(2)}, u32[]{:S(2)}) collective-permute-start(bf16[8,128,256]{2,1,0:T(8,128)(2,1)} %get-tuple-element.39), channel_id=1, source_target_pairs={{0,16},{2,18},{4,20},{6,22},{8,24},{10,26},{12,28},{14,30},{16,0},... | collective-permute-start | bytes 1572872 | tf_op jit(solution)/shard_map/ppermute | solution.py:314
  229.7 27.2 %collective-permute-start.7 = (f32[8,8,128]{2,1,0:T(8,128)}, f32[8,8,128]{2,1,0:T(8,128)S(1)}, u32[]{:S(2)}, u32[]{:S(2)}) collective-permute-start(f32[8,8,128]{2,1,0:T(8,128)} %get-tuple-element.40), channel_id=1, source_target_pairs={{0,16},{2,18},{4,20},{6,22},{8,24},{10,26},{12,28},{14,30},{16,0},... | collective-permute-start | bytes 98312 | tf_op jit(solution)/shard_map/ppermute | solution.py:315
  256.9 0.6 copy-start.8
  256.9 0.8 copy-start.5
  260.5 13.2 %copy-start.1 = (bf16[8,128,256]{2,1,0:T(8,128)(2,1)}, bf16[8,128,256]{2,1,0:T(8,128)(2,1)S(1)}, u32[]{:S(2)}) copy-start(bf16[8,128,256]{2,1,0:T(8,128)(2,1)S(1)} %all-to-all-done.2.refs_0_) | copy-start | bytes 1572868

commit v3 on v2

--- a/solution.py
+++ b/solution.py
@@ -20,32 +20,21 @@
 
 def split_queries(kv_index, queries, members, parts):
     rows = queries.shape[0] // 2
+    group = math.gcd(members, 4)
     width = queries.shape[1] // (members * parts)
 
-    def body(c_ref, q_ref, *rest):
-        outs, sems = rest[:parts], rest[parts]
-        first = pl.multiple_of(c_ref[0] * rows, rows)
-        copies = [
-            pltpu.make_async_copy(
-                q_ref.at[pl.ds(first, rows), pl.ds((j * parts + p) * width, width)], outs[p].at[j], sems.at[p, j]
-            )
-            for p in range(parts)
-            for j in range(members)
-        ]
-        for copy in copies:
-            copy.start()
-        for copy in copies:
-            copy.wait()
-
-    anywhere = pl.BlockSpec(memory_space=pl.ANY)
+    def body(c_ref, q_ref, *outs):
+        for g in range(group):
+            for p in range(parts):
+                outs[p][g] = q_ref[:, pl.ds((g * parts + p) * width, width)]
+
     return pl.pallas_call(
         body,
         grid_spec=pltpu.PrefetchScalarGridSpec(
             num_scalar_prefetch=1,
-            grid=(),
-            in_specs=[anywhere],
-            out_specs=[anywhere] * parts,
-            scratch_shapes=[pltpu.SemaphoreType.DMA((parts, members))],
+            grid=(members // group,),
+            in_specs=[pl.BlockSpec((rows, group * parts * width), lambda j, c: (c[0], j))],
+            out_specs=[pl.BlockSpec((group, rows, width), lambda j, c: (j, 0, 0))] * parts,
         ),
         out_shape=[jax.ShapeDtypeStruct((members, rows, width), queries.dtype)] * parts,
         name="split_queries",
@@ -206,15 +195,12 @@
 
 
 def merge(oa, sa, ob, sb):
-    units, rows, width = oa.shape
-    some = math.gcd(units, 4)
-    o_spec = pl.BlockSpec((some, rows, width), lambda u: (u, 0, 0))
-    s_spec = pl.BlockSpec((some, 8, TILE), lambda u: (u, 0, 0))
-    return pl.pallas_call(
-        functools.partial(merge_kernel, width // DH, some),
-        grid=(units // some,),
-        in_specs=[o_spec, s_spec, o_spec, s_spec],
-        out_specs=o_spec,
+    units, _, width = oa.shape
+    near = pl.BlockSpec(memory_space=pltpu.VMEM)
+    return pl.pallas_call(
+        functools.partial(merge_kernel, width // DH, units),
+        in_specs=[near] * 4,
+        out_specs=near,
         out_shape=jax.ShapeDtypeStruct(oa.shape, oa.dtype),
         name="merge",
     )(oa, sa, ob, sb)
@@ -225,23 +211,16 @@
     members, rows, width = blocks[0].shape
 
     def body(*refs):
-        ins, o_ref, sems = refs[:parts], refs[parts], refs[parts + 1]
-        copies = [
-            pltpu.make_async_copy(ins[p].at[j], o_ref.at[:, pl.ds((j * parts + p) * width, width)], sems.at[p, j])
-            for p in range(parts)
-            for j in range(members)
-        ]
-        for copy in copies:
-            copy.start()
-        for copy in copies:
-            copy.wait()
-
-    anywhere = pl.BlockSpec(memory_space=pl.ANY)
+        o_ref = refs[parts]
+        for j in range(members):
+            for p in range(parts):
+                o_ref[:, pl.ds((j * parts + p) * width, width)] = refs[p][j]
+
+    near = pl.BlockSpec(memory_space=pltpu.VMEM)
     return pl.pallas_call(
         body,
-        in_specs=[anywhere] * parts,
-        out_specs=anywhere,
-        scratch_shapes=[pltpu.SemaphoreType.DMA((parts, members))],
+        in_specs=[near] * parts,
+        out_specs=near,
         out_shape=jax.ShapeDtypeStruct((rows, members * parts * width), blocks[0].dtype),
         name="join_columns",
     )(*blocks)

time: 308 us -> 246 us (0.80)
  Pallas kernels: 154 us -> 92.6 us
    pallas_call x1, Pallas kernels: 33 us -> 2.05 us  [split_queries(): pl.pallas_call(body, grid_spec=pltpu.PrefetchScalarGridSpec(num_scalar_pr...]
    pallas_call x3, Pallas kernels: 38.7 us -> 8.03 us  [the longest x2 5.76 us: merge(): pl.pallas_call(functools.partial(merge_kernel, width // DH, units), in_sp...]
  transfers between devices with their start and end apart: 11 -> 11, of which waited for: 5 -> 5; matrix products, arithmetic and copies ran while one was open for 1% -> 1% of each run, Pallas kernels for 29% -> 36%
where the time goes in v3:
time: 246 us; the launch traced here: 245 us
  Pallas kernels  92.6 us (38%)
  waiting for transfers between devices  73.1 us (30%)
  blocking collectives  52.9 us (22%)
  starting transfers between devices  22.2 us (9%)
  local copies, waits for them, and re-layouts  3.1 us (1%)
    pallas_call x4, Pallas kernels, attend(): pl.pallas_call(functools.partial(attend_kernel, heads, tiles_src), grid_s...  77.5 us
    all_to_all x1, blocking collectives, local(): kv.append(exchange(kv_block))  29.4 us
    ppermute x2, waiting for transfers between devices, local(): s_back = lax.ppermute(s_far, 'head', across)  24.3 us
    all_to_all x1, waiting for transfers between devices, local(): kv.append(exchange(kv_block))  23.1 us
    ppermute x2, waiting for transfers between devices, local(): q_far.append(as_units(lax.ppermute(q_got, 'head', across)))  21.4 us
    all_to_all x1, blocking collectives, local(): blocks.append(exchange(merged.reshape(members, -1, merged.shape[2])))  13.2 us
    all_to_all x1, blocking collectives, local(): q_got = exchange(q_block)  10.4 us
    all_to_all x1, starting transfers between devices, local(): q_got = exchange(q_block)  6.21 us
  transfers between devices with their start and end apart: 11, of which 5 were waited for; matrix products, arithmetic and copies ran while one was open for 1% of the time, Pallas kernels for 36%

profile of v3, /device:TPU:0, one launch (start us, length us, event | category | flops | bytes accessed | tf_op | source)
XLA Modules:
  0.0 245.0 jit_solution(10518556909845425776)
XLA Ops:
  0.0 2.1 split_queries.1
  2.1 6.2 %all-to-all-start = ((bf16[8,128,256]{2,1,0:T(8,128)(2,1)}), bf16[8,128,256]{2,1,0:T(8,128)(2,1)S(1)}, u32[]{:S(2)}, u32[]{:S(2)}) async-start(bf16[8,128,256]{2,1,0:T(8,128)(2,1)} %get-tuple-element.23), calls=%async_computation | async-start | bytes 1048576 | tf_op jit(solution)/shard_map/all_to_all | solution.py:283
  8.3 5.0 %split_keys.1 = (bf16[8,2,4,128,128]{4,3,2,1,0:T(8,128)(2,1)}, bf16[8,2,4,128,128]{4,3,2,1,0:T(8,128)(2,1)}) custom-call(bf16[256,4096]{1,0:T(8,128)(2,1)} %k_ref.1, bf16[256,4096]{1,0:T(8,128)(2,1)} %v_ref.1), custom_call_target="tpu_custom_call" | custom-call | tf_op jit(solution)/shard_map/split_keys/pallas_call | solution.py:61
  13.2 4.2 %all-to-all-done.q_ref = bf16[8,128,256]{2,1,0:T(8,128)(2,1)S(1)} async-done(((bf16[8,128,256]{2,1,0:T(8,128)(2,1)}), bf16[8,128,256]{2,1,0:T(8,128)(2,1)S(1)}, u32[]{:S(2)}, u32[]{:S(2)}) %all-to-all-start) | async-done | bytes 524320 | tf_op jit(solution)/shard_map/all_to_all | solution.py:283
  17.4 29.4 %all_to_all.30 = bf16[8,2,4,128,128]{4,3,2,1,0:T(8,128)(2,1)} all-to-all(bf16[8,2,4,128,128]{4,3,2,1,0:T(8,128)(2,1)} %get-tuple-element.26), channel_id=1, replica_groups={{0,2,4,6,8,10,12,14},{16,18,20,22,24,26,28,30},{1,3,5,7,9,11,13,15},{17..., dimensions={0} | all-to-all | bytes 4194304 | tf_op jit(solution)/shard_map/all_to_all | solution.py:287
  46.7 10.4 %all_to_all.31.q_ref = bf16[8,128,256]{2,1,0:T(8,128)(2,1)S(1)} all-to-all(bf16[8,128,256]{2,1,0:T(8,128)(2,1)S(1)} %copy-done.6), channel_id=1, replica_groups={{0,2,4,6,8,10,12,14},{16,18,20,22,24,26,28,30},{1,3,5,7,9,11,13,15},{17..., dimensions={0} | all-to-all | bytes 1048576 | tf_op jit(solution)/shard_map/all_to_all | solution.py:283
  57.2 3.7 %all-to-all-start.4 = ((bf16[8,2,4,128,128]{4,3,2,1,0:T(8,128)(2,1)}), bf16[8,2,4,128,128]{4,3,2,1,0:T(8,128)(2,1)S(1)}, u32[]{:S(2)}, u32[]{:S(2)}) async-start(bf16[8,2,4,128,128]{4,3,2,1,0:T(8,128)(2,1)} %get-tuple-element.36), calls=%async_computation.4 | async-start | bytes 4194304 | tf_op jit(solution)/shard_map/all_to_all | solution.py:287
  61.0 23.1 %all-to-all-done.4 = bf16[8,2,4,128,128]{4,3,2,1,0:T(8,128)(2,1)S(1)} async-done(((bf16[8,2,4,128,128]{4,3,2,1,0:T(8,128)(2,1)}), bf16[8,2,4,128,128]{4,3,2,1,0:T(8,128)(2,1)S(1)}, u32[]{:S(2)}, u32[]{:S(2)}) %all-to-all-start.4) | async-done | bytes 2097184 | tf_op jit(solution)/shard_map/all_to_all | solution.py:287
  84.1 2.7 %collective-permute-start.1 = (bf16[8,128,256]{2,1,0:T(8,128)(2,1)S(1)}, bf16[8,128,256]{2,1,0:T(8,128)(2,1)}, u32[]{:S(2)}, u32[]{:S(2)}) collective-permute-start(bf16[8,128,256]{2,1,0:T(8,128)(2,1)S(1)} %all-to-all-done.q_ref), channel_id=1, source_target_pairs={{0,16},{2,18},{4,20},{6,22},{8,24},{10,26},{12,28},{14,30},{16,0},... | collective-permute-start | bytes 1572872 | tf_op jit(solution)/shard_map/ppermute | solution.py:286
  87.1 0.8 dynamic-slice_reduce_fusion
  89.3 21.4 %collective-permute-done.1.q_ref = bf16[8,128,256]{2,1,0:T(8,128)(2,1)} collective-permute-done((bf16[8,128,256]{2,1,0:T(8,128)(2,1)S(1)}, bf16[8,128,256]{2,1,0:T(8,128)(2,1)}, u32[]{:S(2)}, u32[]{:S(2)}) %collective-permute-start.1) | collective-permute-done | bytes 524320 | tf_op jit(solution)/shard_map/ppermute | solution.py:286
  110.7 15.5 %attend.5 = (bf16[8,128,256]{2,1,0:T(8,128)(2,1)}, f32[8,8,128]{2,1,0:T(8,128)}) custom-call(s32[8,32]{1,0:T(8,128)} %bitcast.15, s32[8]{0:T(128)} %get-tuple-element.41.counts_ref, bf16[8,128,256]{2,1,0:T(8,128)(2,1)} %collective-permute-done.1.q_ref, bf16[16,4,128,128]{3,2,1,0:T(8,128)(2,1)} %bitcast.10, bf16[16,4,128,128]{3,2,1,0:T(8,128)(2,1)} %bitcast.4.far_ref), custom_call_target="tpu_custom_call" | custom-call | tf_op jit(solution)/shard_map/attend/pallas_call | solution.py:171
  126.3 2.9 %collective-permute-start.5 = (bf16[8,128,256]{2,1,0:T(8,128)(2,1)S(1)}, bf16[8,128,256]{2,1,0:T(8,128)(2,1)}, u32[]{:S(2)}, u32[]{:S(2)}) collective-permute-start(bf16[8,128,256]{2,1,0:T(8,128)(2,1)S(1)} %all_to_all.31.q_ref), channel_id=1, source_target_pairs={{0,16},{2,18},{4,20},{6,22},{8,24},{10,26},{12,28},{14,30},{16,0},... | collective-permute-start | bytes 1572872 | tf_op jit(solution)/shard_map/ppermute | solution.py:286
  129.3 23.3 %attend.4 = (bf16[8,128,256]{2,1,0:T(8,128)(2,1)}, f32[8,8,128]{2,1,0:T(8,128)}) custom-call(s32[8,32]{1,0:T(8,128)} %bitcast.13, s32[8]{0:T(128)} %get-tuple-element.42.counts_ref, bf16[8,128,256]{2,1,0:T(8,128)(2,1)} %copy-done.3, bf16[16,4,128,128]{3,2,1,0:T(8,128)(2,1)} %bitcast.11, bf16[16,4,128,128]{3,2,1,0:T(8,128)(2,1)} %bitcast.4.far_ref), custom_call_target="tpu_custom_call" | custom-call | tf_op jit(solution)/shard_map/attend/pallas_call | solution.py:171
  152.6 22.9 %collective-permute-done.3.sb_ref = f32[8,8,128]{2,1,0:T(8,128)S(1)} collective-permute-done((f32[8,8,128]{2,1,0:T(8,128)}, f32[8,8,128]{2,1,0:T(8,128)S(1)}, u32[]{:S(2)}, u32[]{:S(2)}) %collective-permute-start.3) | collective-permute-done | bytes 32800 | tf_op jit(solution)/shard_map/ppermute | solution.py:294
  176.3 2.9 %merge.2 = bf16[8,128,256]{2,1,0:T(8,128)(2,1)} custom-call(bf16[8,128,256]{2,1,0:T(8,128)(2,1)} %get-tuple-element.29.oa_ref, f32[8,8,128]{2,1,0:T(8,128)} %get-tuple-element.30.sa_ref, bf16[8,128,256]{2,1,0:T(8,128)(2,1)} %copy-done.4, f32[8,8,128]{2,1,0:T(8,128)} %copy-done.7), custom_call_target="tpu_custom_call" | custom-call | tf_op jit(solution)/shard_map/merge/pallas_call | solution.py:200
  179.2 3.5 %all-to-all-start.2 = ((bf16[8,128,256]{2,1,0:T(8,128)(2,1)}), bf16[8,128,256]{2,1,0:T(8,128)(2,1)S(1)}, u32[]{:S(2)}, u32[]{:S(2)}) async-start(bf16[8,128,256]{2,1,0:T(8,128)(2,1)} %merge.2), calls=%async_computation.2 | async-start | bytes 1048576 | tf_op jit(solution)/shard_map/all_to_all | solution.py:297
  182.7 15.5 %attend.7 = (bf16[8,128,256]{2,1,0:T(8,128)(2,1)}, f32[8,8,128]{2,1,0:T(8,128)}) custom-call(s32[8,32]{1,0:T(8,128)} %bitcast.16, s32[8]{0:T(128)} %get-tuple-element.41.counts_ref, bf16[8,128,256]{2,1,0:T(8,128)(2,1)} %collective-permute-done.5.q_ref, bf16[16,4,128,128]{3,2,1,0:T(8,128)(2,1)} %bitcast.8, bf16[16,4,128,128]{3,2,1,0:T(8,128)(2,1)} %bitcast.7.far_ref), custom_call_target="tpu_custom_call" | custom-call | tf_op jit(solution)/shard_map/attend/pallas_call | solution.py:171
  198.7 2.5 %collective-permute-start.7 = (f32[8,8,128]{2,1,0:T(8,128)}, f32[8,8,128]{2,1,0:T(8,128)S(1)}, u32[]{:S(2)}, u32[]{:S(2)}) collective-permute-start(f32[8,8,128]{2,1,0:T(8,128)} %get-tuple-element.40), channel_id=1, source_target_pairs={{0,16},{2,18},{4,20},{6,22},{8,24},{10,26},{12,28},{14,30},{16,0},... | collective-permute-start | bytes 98312 | tf_op jit(solution)/shard_map/ppermute | solution.py:294
  201.2 23.2 %attend.6 = (bf16[8,128,256]{2,1,0:T(8,128)(2,1)}, f32[8,8,128]{2,1,0:T(8,128)}) custom-call(s32[8,32]{1,0:T(8,128)} %bitcast.14, s32[8]{0:T(128)} %get-tuple-element.42.counts_ref, bf16[8,128,256]{2,1,0:T(8,128)(2,1)} %copy-done.2, bf16[16,4,128,128]{3,2,1,0:T(8,128)(2,1)} %bitcast.9, bf16[16,4,128,128]{3,2,1,0:T(8,128)(2,1)} %bitcast.7.far_ref), custom_call_target="tpu_custom_call" | custom-call | tf_op jit(solution)/shard_map/attend/pallas_call | solution.py:171
  224.5 1.4 collective-permute-done.7.sb_ref
  226.7 2.9 %merge.3 = bf16[8,128,256]{2,1,0:T(8,128)(2,1)} custom-call(bf16[8,128,256]{2,1,0:T(8,128)(2,1)} %get-tuple-element.37.oa_ref, f32[8,8,128]{2,1,0:T(8,128)} %get-tuple-element.38.sa_ref, bf16[8,128,256]{2,1,0:T(8,128)(2,1)} %copy-done.5, f32[8,8,128]{2,1,0:T(8,128)} %copy-done.8), custom_call_target="tpu_custom_call" | custom-call | tf_op jit(solution)/shard_map/merge/pallas_call | solution.py:200
  229.6 13.2 %all_to_all.32.refs_1_ = bf16[8,128,256]{2,1,0:T(8,128)(2,1)} all-to-all(bf16[8,128,256]{2,1,0:T(8,128)(2,1)} %merge.3), channel_id=1, replica_groups={{0,2,4,6,8,10,12,14},{16,18,20,22,24,26,28,30},{1,3,5,7,9,11,13,15},{17..., dimensions={0} | all-to-all | bytes 1048576 | tf_op jit(solution)/shard_map/all_to_all | solution.py:297
  242.7 2.3 join_columns.1
  (38 shorter events, 4.0 us)
Async XLA Ops:
  2.1 15.3 %all-to-all-start = ((bf16[8,128,256]{2,1,0:T(8,128)(2,1)}), bf16[8,128,256]{2,1,0:T(8,128)(2,1)S(1)}, u32[]{:S(2)}, u32[]{:S(2)}) async-start(bf16[8,128,256]{2,1,0:T(8,128)(2,1)} %get-tuple-element.23), calls=%async_computation | async-start | bytes 1048576 | tf_op jit(solution)/shard_map/all_to_all | solution.py:283
  17.4 66.8 %copy-start.3 = (bf16[8,128,256]{2,1,0:T(8,128)(2,1)}, bf16[8,128,256]{2,1,0:T(8,128)(2,1)S(1)}, u32[]{:S(2)}) copy-start(bf16[8,128,256]{2,1,0:T(8,128)(2,1)S(1)} %all-to-all-done.q_ref) | copy-start | bytes 1572868
  17.4 29.4 %copy-start.6 = (bf16[8,128,256]{2,1,0:T(8,128)(2,1)S(1)}, bf16[8,128,256]{2,1,0:T(8,128)(2,1)}, u32[]{:S(2)}) copy-start(bf16[8,128,256]{2,1,0:T(8,128)(2,1)} %get-tuple-element.33) | copy-start | bytes 1572868
  57.2 69.1 %copy-start.2 = (bf16[8,128,256]{2,1,0:T(8,128)(2,1)}, bf16[8,128,256]{2,1,0:T(8,128)(2,1)S(1)}, u32[]{:S(2)}) copy-start(bf16[8,128,256]{2,1,0:T(8,128)(2,1)S(1)} %all_to_all.31.q_ref) | copy-start | bytes 1572868
  57.2 29.6 %copy-start.9 = (s32[32,32]{1,0:T(8,128)S(1)}, s32[32,32]{1,0:T(8,128)}, u32[]{:S(2)}) copy-start(s32[32,32]{1,0:T(8,128)} %param.7) | copy-start | bytes 12292
  57.2 27.0 %all-to-all-start.4 = ((bf16[8,2,4,128,128]{4,3,2,1,0:T(8,128)(2,1)}), bf16[8,2,4,128,128]{4,3,2,1,0:T(8,128)(2,1)S(1)}, u32[]{:S(2)}, u32[]{:S(2)}) async-start(bf16[8,2,4,128,128]{4,3,2,1,0:T(8,128)(2,1)} %get-tuple-element.36), calls=%async_computation.4 | async-start | bytes 4194304 | tf_op jit(solution)/shard_map/all_to_all | solution.py:287
  60.9 49.8 %collective-permute-start = (bf16[8,2,4,128,128]{4,3,2,1,0:T(8,128)(2,1)}, bf16[8,2,4,128,128]{4,3,2,1,0:T(8,128)(2,1)}, u32[]{:S(2)}, u32[]{:S(2)}) collective-permute-start(bf16[8,2,4,128,128]{4,3,2,1,0:T(8,128)(2,1)} %all_to_all.30), channel_id=1, source_target_pairs={{0,1},{1,0},{2,3},{3,2},{4,5},{5,4},{6,7},{7,6},{8,9},{9,8},{10,11... | collective-permute-start | bytes 6291464 | tf_op jit(solution)/shard_map/ppermute | solution.py:291
  84.1 42.1 %copy-start = (bf16[8,2,4,128,128]{4,3,2,1,0:T(8,128)(2,1)}, bf16[8,2,4,128,128]{4,3,2,1,0:T(8,128)(2,1)S(1)}, u32[]{:S(2)}) copy-start(bf16[8,2,4,128,128]{4,3,2,1,0:T(8,128)(2,1)S(1)} %all-to-all-done.4) | copy-start | bytes 6291460
  84.1 98.6 %collective-permute-start.4 = (bf16[8,2,4,128,128]{4,3,2,1,0:T(8,128)(2,1)S(1)}, bf16[8,2,4,128,128]{4,3,2,1,0:T(8,128)(2,1)}, u32[]{:S(2)}, u32[]{:S(2)}) collective-permute-start(bf16[8,2,4,128,128]{4,3,2,1,0:T(8,128)(2,1)S(1)} %all-to-all-done.4), channel_id=1, source_target_pairs={{0,1},{1,0},{2,3},{3,2},{4,5},{5,4},{6,7},{7,6},{8,9},{9,8},{10,11... | collective-permute-start | bytes 6291464 | tf_op jit(solution)/shard_map/ppermute | solution.py:291
  84.1 26.6 %collective-permute-start.1 = (bf16[8,128,256]{2,1,0:T(8,128)(2,1)S(1)}, bf16[8,128,256]{2,1,0:T(8,128)(2,1)}, u32[]{:S(2)}, u32[]{:S(2)}) collective-permute-start(bf16[8,128,256]{2,1,0:T(8,128)(2,1)S(1)} %all-to-all-done.q_ref), channel_id=1, source_target_pairs={{0,16},{2,18},{4,20},{6,22},{8,24},{10,26},{12,28},{14,30},{16,0},... | collective-permute-start | bytes 1572872 | tf_op jit(solution)/shard_map/ppermute | solution.py:286
  126.2 49.3 %collective-permute-start.2 = (bf16[8,128,256]{2,1,0:T(8,128)(2,1)}, bf16[8,128,256]{2,1,0:T(8,128)(2,1)S(1)}, u32[]{:S(2)}, u32[]{:S(2)}) collective-permute-start(bf16[8,128,256]{2,1,0:T(8,128)(2,1)} %get-tuple-element.31), channel_id=1, source_target_pairs={{0,16},{2,18},{4,20},{6,22},{8,24},{10,26},{12,28},{14,30},{16,0},... | collective-permute-start | bytes 1572872 | tf_op jit(solution)/shard_map/ppermute | solution.py:293
  126.3 56.4 %collective-permute-start.5 = (bf16[8,128,256]{2,1,0:T(8,128)(2,1)S(1)}, bf16[8,128,256]{2,1,0:T(8,128)(2,1)}, u32[]{:S(2)}, u32[]{:S(2)}) collective-permute-start(bf16[8,128,256]{2,1,0:T(8,128)(2,1)S(1)} %all_to_all.31.q_ref), channel_id=1, source_target_pairs={{0,16},{2,18},{4,20},{6,22},{8,24},{10,26},{12,28},{14,30},{16,0},... | collective-permute-start | bytes 1572872 | tf_op jit(solution)/shard_map/ppermute | solution.py:286
  129.2 46.3 %collective-permute-start.3 = (f32[8,8,128]{2,1,0:T(8,128)}, f32[8,8,128]{2,1,0:T(8,128)S(1)}, u32[]{:S(2)}, u32[]{:S(2)}) collective-permute-start(f32[8,8,128]{2,1,0:T(8,128)} %get-tuple-element.32), channel_id=1, source_target_pairs={{0,16},{2,18},{4,20},{6,22},{8,24},{10,26},{12,28},{14,30},{16,0},... | collective-permute-start | bytes 98312 | tf_op jit(solution)/shard_map/ppermute | solution.py:294
  175.5 0.6 copy-start.7
  175.5 0.8 copy-start.4
  179.2 50.4 %all-to-all-start.2 = ((bf16[8,128,256]{2,1,0:T(8,128)(2,1)}), bf16[8,128,256]{2,1,0:T(8,128)(2,1)S(1)}, u32[]{:S(2)}, u32[]{:S(2)}) async-start(bf16[8,128,256]{2,1,0:T(8,128)(2,1)} %merge.2), calls=%async_computation.2 | async-start | bytes 1048576 | tf_op jit(solution)/shard_map/all_to_all | solution.py:297
  198.2 27.7 %collective-permute-start.6 = (bf16[8,128,256]{2,1,0:T(8,128)(2,1)}, bf16[8,128,256]{2,1,0:T(8,128)(2,1)S(1)}, u32[]{:S(2)}, u32[]{:S(2)}) collective-permute-start(bf16[8,128,256]{2,1,0:T(8,128)(2,1)} %get-tuple-element.39), channel_id=1, source_target_pairs={{0,16},{2,18},{4,20},{6,22},{8,24},{10,26},{12,28},{14,30},{16,0},... | collective-permute-start | bytes 1572872 | tf_op jit(solution)/shard_map/ppermute | solution.py:293
  198.7 27.2 %collective-permute-start.7 = (f32[8,8,128]{2,1,0:T(8,128)}, f32[8,8,128]{2,1,0:T(8,128)S(1)}, u32[]{:S(2)}, u32[]{:S(2)}) collective-permute-start(f32[8,8,128]{2,1,0:T(8,128)} %get-tuple-element.40), channel_id=1, source_target_pairs={{0,16},{2,18},{4,20},{6,22},{8,24},{10,26},{12,28},{14,30},{16,0},... | collective-permute-start | bytes 98312 | tf_op jit(solution)/shard_map/ppermute | solution.py:294
  225.9 0.6 copy-start.8
  225.9 0.8 copy-start.5
  229.6 13.2 %copy-start.1 = (bf16[8,128,256]{2,1,0:T(8,128)(2,1)}, bf16[8,128,256]{2,1,0:T(8,128)(2,1)S(1)}, u32[]{:S(2)}) copy-start(bf16[8,128,256]{2,1,0:T(8,128)(2,1)S(1)} %all-to-all-done.2.refs_0_) | copy-start | bytes 1572868

commit v4 on v3

--- a/solution.py
+++ b/solution.py
@@ -12,31 +12,30 @@
 HEADS = 32
 DH = 128
 TILE = 128
-STEP = 8
+STEP = 6
 GROUPS = 2
 LOW = -1e30
 SCALE = math.log2(math.e) / math.sqrt(DH)
 
 
-def split_queries(kv_index, queries, members, parts):
+def split_queries(kv_index, queries, members):
     rows = queries.shape[0] // 2
     group = math.gcd(members, 4)
-    width = queries.shape[1] // (members * parts)
-
-    def body(c_ref, q_ref, *outs):
+    width = queries.shape[1] // members
+
+    def body(c_ref, q_ref, o_ref):
         for g in range(group):
-            for p in range(parts):
-                outs[p][g] = q_ref[:, pl.ds((g * parts + p) * width, width)]
+            o_ref[g] = q_ref[:, pl.ds(g * width, width)]
 
     return pl.pallas_call(
         body,
         grid_spec=pltpu.PrefetchScalarGridSpec(
             num_scalar_prefetch=1,
             grid=(members // group,),
-            in_specs=[pl.BlockSpec((rows, group * parts * width), lambda j, c: (c[0], j))],
-            out_specs=[pl.BlockSpec((group, rows, width), lambda j, c: (j, 0, 0))] * parts,
+            in_specs=[pl.BlockSpec((rows, group * width), lambda j, c: (c[0], j))],
+            out_specs=pl.BlockSpec((group, rows, width), lambda j, c: (j, 0, 0)),
         ),
-        out_shape=[jax.ShapeDtypeStruct((members, rows, width), queries.dtype)] * parts,
+        out_shape=jax.ShapeDtypeStruct((members, rows, width), queries.dtype),
         name="split_queries",
     )(kv_index.reshape(1), queries)
 
@@ -70,79 +69,91 @@
 
 def attend_kernel(
     heads, tiles_src, lists_ref, counts_ref, q_ref, near_ref, far_ref, o_ref, st_ref,
-    kv_scr, m_scr, l_scr, acc_scr, sems,
+    kv_scr, s_scr, p_scr, peak_scr, m_scr, l_scr, alpha_scr, acc_scr, sems,
 ):
-    unit = pl.program_id(0)
-
-    @pl.when(unit == 0)
-    def _():
-        copies = [
-            pltpu.make_async_copy(src, kv_scr.at[pl.ds(n * tiles_src, tiles_src)], sems.at[n])
-            for n, src in enumerate((near_ref, far_ref))
-        ]
-        for copy in copies:
-            copy.start()
-        for copy in copies:
-            copy.wait()
-
-    count = counts_ref[unit]
+    units = q_ref.shape[0]
+    blank = 2 * tiles_src
+    copies = [
+        pltpu.make_async_copy(src, kv_scr.at[pl.ds(n * tiles_src, tiles_src)], sems.at[n])
+        for n, src in enumerate((near_ref, far_ref))
+    ]
+    for copy in copies:
+        copy.start()
+    kv_scr[blank] = jnp.zeros_like(kv_scr[blank])
+    p_scr[...] = jnp.zeros_like(p_scr)
     m_scr[...] = jnp.full_like(m_scr, LOW)
     l_scr[...] = jnp.zeros_like(l_scr)
+    alpha_scr[...] = jnp.zeros_like(alpha_scr)
     acc_scr[...] = jnp.zeros_like(acc_scr)
-
-    def step(first, size, masked):
-        ids = [lists_ref[unit, first + n] for n in range(size)]
-        scores = []
+    for copy in copies:
+        copy.wait()
+
+    def score(unit, first):
+        count = counts_ref[unit]
+        ids = [lists_ref[unit, jnp.where(first + n < count, first + n, 0)] for n in range(STEP)]
         for h in range(heads):
             k_block = jnp.concatenate([kv_scr[t, h] for t in ids], axis=0)
-            scores.append(
-                lax.dot_general(
-                    k_block, q_ref[0, :, pl.ds(h * DH, DH)], (((1,), (1,)), ((), ())),
-                    preferred_element_type=jnp.float32,
-                )
+            found = lax.dot_general(
+                k_block, q_ref[unit, :, pl.ds(h * DH, DH)], (((1,), (1,)), ((), ())),
+                preferred_element_type=jnp.float32,
             )
-        if masked:
-            slot = first + lax.broadcasted_iota(jnp.int32, (size * TILE, 1), 0) // TILE
-            valid = slot < count
+            s_scr[h] = found
+            peak_scr[h] = jnp.max(found.reshape(-1, 8, TILE), axis=0)
+
+    def weigh(unit, first):
+        count = counts_ref[unit]
         for h in range(heads):
-            score = jnp.where(valid, scores[h], LOW) if masked else scores[h]
-            m_old = m_scr[h]
-            peak = jnp.max(jnp.max(score.reshape(-1, 8, TILE), axis=0), axis=0, keepdims=True)
-            m_new = jnp.maximum(m_old, peak)
+            m_old = jnp.where(first == 0, LOW, m_scr[h])
+            m_new = jnp.maximum(m_old, jnp.max(peak_scr[h], axis=0, keepdims=True))
+            alpha = jnp.exp2((m_old - m_new) * SCALE)
             m_scr[h] = m_new
-            expo = jnp.exp2((score - m_new[:1]) * SCALE)
-            if masked:
-                expo = jnp.where(valid, expo, 0.0)
-            alpha = jnp.exp2((m_old - m_new) * SCALE)
-            l_scr[h] = l_scr[h] * alpha + jnp.sum(expo.reshape(-1, 8, TILE), axis=0)
+            alpha_scr[h] = alpha
+            total = l_scr[h] * alpha
+            for n in range(STEP):
+                rows = pl.ds(n * TILE, TILE)
+                expo = jnp.exp2((s_scr[h, rows] - m_new[:1]) * SCALE)
+                p_scr[h, rows] = expo.astype(jnp.bfloat16)
+                part = jnp.sum(expo.reshape(-1, 8, TILE), axis=0)
+                total = total + jnp.where(first + n < count, part, 0.0)
+            l_scr[h] = total
+
+    def gather(unit, first):
+        count = counts_ref[unit]
+        ids = [jnp.where(first + n < count, lists_ref[unit, jnp.minimum(first + n, lists_ref.shape[1] - 1)], blank)
+               for n in range(STEP)]
+        for h in range(heads):
             v_block = jnp.concatenate([kv_scr[t, heads + h] for t in ids], axis=1)
-            acc_scr[h] = acc_scr[h] * alpha[:1] + jnp.dot(
-                v_block, expo.astype(jnp.bfloat16), preferred_element_type=jnp.float32
-            )
-
-    full = count // STEP
-    rest = count - full * STEP
-
-    def loop_body(i, carry):
-        step(i * STEP, STEP, False)
-        return carry
-
-    lax.fori_loop(0, full, loop_body, 0)
-
-    @pl.when(rest > STEP // 2)
-    def _():
-        step(full * STEP, STEP, True)
-
-    @pl.when((rest > 0) & (rest <= STEP // 2))
-    def _():
-        step(full * STEP, STEP // 2, True)
-
-    for h in range(heads):
-        total = jnp.sum(l_scr[h], axis=0, keepdims=True)
-        some = total > 0.0
-        safe = jnp.where(some, total, 1.0)
-        o_ref[0, :, pl.ds(h * DH, DH)] = (acc_scr[h] * (1.0 / safe)).astype(o_ref.dtype).T
-        st_ref[0, h : h + 1] = jnp.where(some, m_scr[h][:1] * SCALE + jnp.log2(safe), LOW)
+            acc = acc_scr[h] * alpha_scr[h, :1] + jnp.dot(v_block, p_scr[h], preferred_element_type=jnp.float32)
+            acc_scr[h] = acc
+            total = jnp.sum(l_scr[h], axis=0, keepdims=True)
+            some = total > 0.0
+            safe = jnp.where(some, total, 1.0)
+            o_ref[unit, :, pl.ds(h * DH, DH)] = (acc * (1.0 / safe)).astype(o_ref.dtype).T
+            st_ref[unit, h : h + 1] = jnp.where(some, m_scr[h, :1] * SCALE + jnp.log2(safe), LOW)
+
+    zero = jnp.int32(0)
+    steps = lax.fori_loop(
+        0, units, lambda u, n: n + jnp.maximum((counts_ref[u] + (STEP - 1)) // STEP, 1), zero
+    )
+
+    def following(unit, first):
+        more = first + STEP < counts_ref[unit]
+        return (
+            jnp.where(more, unit, jnp.minimum(unit + 1, units - 1)),
+            jnp.where(more, first + STEP, 0),
+        )
+
+    def body(i, carry):
+        before, now = carry
+        later = following(*now)
+        gather(*before)
+        weigh(*now)
+        score(*later)
+        return now, later
+
+    score(zero, zero)
+    last, _ = lax.fori_loop(0, steps, body, ((zero, zero), (zero, zero)))
+    gather(*last)
 
 
 def attend(lists, counts, q, kv_near, kv_far):
@@ -152,25 +163,23 @@
     kv_near, kv_far = as_tiles(kv_near), as_tiles(kv_far)
     tiles_src = kv_near.shape[0]
     anywhere = pl.BlockSpec(memory_space=pl.ANY)
-    grid_spec = pltpu.PrefetchScalarGridSpec(
-        num_scalar_prefetch=2,
-        grid=(units,),
-        in_specs=[pl.BlockSpec((1, rows, width), lambda u, *_: (u, 0, 0))] + [anywhere] * 2,
-        out_specs=[
-            pl.BlockSpec((1, rows, width), lambda u, *_: (u, 0, 0)),
-            pl.BlockSpec((1, 8, TILE), lambda u, *_: (u, 0, 0)),
-        ],
+    near = pl.BlockSpec(memory_space=pltpu.VMEM)
+    scalars = pl.BlockSpec(memory_space=pltpu.SMEM)
+    return pl.pallas_call(
+        functools.partial(attend_kernel, heads, tiles_src),
+        in_specs=[scalars, scalars, near, anywhere, anywhere],
+        out_specs=[near, near],
         scratch_shapes=[
-            pltpu.VMEM((2 * tiles_src, 2 * heads, TILE, DH), jnp.bfloat16),
+            pltpu.VMEM((2 * tiles_src + 1, 2 * heads, TILE, DH), jnp.bfloat16),
+            pltpu.VMEM((heads, STEP * TILE, TILE), jnp.float32),
+            pltpu.VMEM((heads, STEP * TILE, TILE), jnp.bfloat16),
+            pltpu.VMEM((heads, 8, TILE), jnp.float32),
+            pltpu.VMEM((heads, 8, TILE), jnp.float32),
             pltpu.VMEM((heads, 8, TILE), jnp.float32),
             pltpu.VMEM((heads, 8, TILE), jnp.float32),
             pltpu.VMEM((heads, DH, TILE), jnp.float32),
             pltpu.SemaphoreType.DMA((2,)),
         ],
-    )
-    return pl.pallas_call(
-        functools.partial(attend_kernel, heads, tiles_src),
-        grid_spec=grid_spec,
         out_shape=[
             jax.ShapeDtypeStruct((units, rows, width), jnp.bfloat16),
             jax.ShapeDtypeStruct((units, 8, TILE), jnp.float32),
@@ -271,19 +280,21 @@
 
     far_lists, near_lists = lists_of(1 - group), lists_of(group)
 
-    as_units = lambda t: t.reshape(units, TILE, t.shape[2])
-    q_blocks = split_queries(kv_index, queries, members, parts)
-    kv_blocks = list(split_keys(keys, values, members, parts))
+    q_blocks = split_queries(kv_index, queries, members)
+    (far_lists, near_lists), keys = then((far_lists, near_lists), keys)
+    kv_blocks = split_keys(keys, values, members, parts)
+    q_got = exchange(q_blocks)
+    q_got, kv_blocks = then(q_got, list(kv_blocks))
+    q_units = q_got.reshape(units, TILE, -1)
+    width = q_units.shape[2] // parts
 
     q_near, q_far, kv = [], [], []
     for p in range(parts):
-        q_block, kv_block = q_blocks[p], kv_blocks[p]
+        q_near.append(q_units[:, :, p * width : (p + 1) * width])
+        q_far.append(lax.ppermute(q_near[p], "head", across))
+        kv_block = kv_blocks[p]
         if p:
-            kv[p - 1], q_block = then(kv[p - 1], q_block)
-        q_got = exchange(q_block)
-        q_got, kv_block = then(q_got, kv_block)
-        q_near.append(as_units(q_got))
-        q_far.append(as_units(lax.ppermute(q_got, "head", across)))
+            kv[p - 1], kv_block = then(kv[p - 1], kv_block)
         kv.append(exchange(kv_block))
 
     blocks = []

time: 246 us -> 235 us (0.955)
  Pallas kernels: 92.6 us -> 72.6 us
  waiting for transfers between devices: 73.1 us -> 90 us
  blocking collectives: 52.9 us -> 43.4 us
    pallas_call x4, Pallas kernels: 77.5 us -> 57.6 us  [attend(): pl.pallas_call(functools.partial(attend_kernel, heads, tiles_src), in_spe...]
    all_to_all x1 -> x0, blocking collectives: 10.4 us -> none  [local(): q_got = exchange(q_block)]
    ppermute x2, waiting for transfers between devices: 24.3 us -> 34.3 us  [local(): s_back = lax.ppermute(s_far, 'head', across)]
    all_to_all x1, waiting for transfers between devices: 4.16 us -> 7.23 us  [local(): q_got = exchange(q_blocks)]
  transfers between devices with their start and end apart: 11 -> 11, of which waited for: 5 -> 5; matrix products, arithmetic and copies ran while one was open for 1% -> 1% of each run, Pallas kernels for 36% -> 29%
where the time goes in v4:
time: 235 us; the launch traced here: 234 us
  waiting for transfers between devices  90 us (38%)
  Pallas kernels  72.6 us (31%)
  blocking collectives  43.4 us (18%)
  starting transfers between devices  22 us (9%)
  local copies, waits for them, and re-layouts  4.97 us (2%)
    pallas_call x4, Pallas kernels, attend(): pl.pallas_call(functools.partial(attend_kernel, heads, tiles_src), in_spe...  57.6 us
    ppermute x2, waiting for transfers between devices, local(): s_back = lax.ppermute(s_far, 'head', across)  34.3 us
    all_to_all x1, blocking collectives, local(): kv.append(exchange(kv_block))  29.8 us
    all_to_all x1, waiting for transfers between devices, local(): kv.append(exchange(kv_block))  24.7 us
    ppermute x2, waiting for transfers between devices, local(): q_far.append(lax.ppermute(q_near[p], 'head', across))  23.8 us
    all_to_all x1, blocking collectives, local(): blocks.append(exchange(merged.reshape(members, -1, merged.shape[2])))  13.7 us
    all_to_all x1, waiting for transfers between devices, local(): q_got = exchange(q_blocks)  7.23 us
    all_to_all x1, starting transfers between devices, local(): q_got = exchange(q_blocks)  6.21 us
  transfers between devices with their start and end apart: 11, of which 5 were waited for; matrix products, arithmetic and copies ran while one was open for 1% of the time, Pallas kernels for 29%

profile of v4, /device:TPU:0, one launch (start us, length us, event | category | flops | bytes accessed | tf_op | source)
XLA Modules:
  0.0 234.2 jit_solution(3917521653665413184)
XLA Ops:
  0.0 2.1 split_queries.1
  2.1 6.2 %all-to-all-start = ((bf16[8,128,512]{2,1,0:T(8,128)(2,1)}), bf16[8,128,512]{2,1,0:T(8,128)(2,1)S(1)}, u32[]{:S(2)}, u32[]{:S(2)}) async-start(bf16[8,128,512]{2,1,0:T(8,128)(2,1)} %split_queries.1), calls=%async_computation | async-start | bytes 2097152 | tf_op jit(solution)/shard_map/all_to_all | solution.py:286
  10.8 4.9 %split_keys.1 = (bf16[8,2,4,128,128]{4,3,2,1,0:T(8,128)(2,1)}, bf16[8,2,4,128,128]{4,3,2,1,0:T(8,128)(2,1)}) custom-call(bf16[256,4096]{1,0:T(8,128)(2,1)} %k_ref, bf16[256,4096]{1,0:T(8,128)(2,1)} %v_ref.1), custom_call_target="tpu_custom_call" | custom-call | tf_op jit(solution)/shard_map/split_keys/pallas_call | solution.py:60
  15.7 7.2 %all-to-all-done = bf16[8,128,512]{2,1,0:T(8,128)(2,1)S(1)} async-done(((bf16[8,128,512]{2,1,0:T(8,128)(2,1)}), bf16[8,128,512]{2,1,0:T(8,128)(2,1)S(1)}, u32[]{:S(2)}, u32[]{:S(2)}) %all-to-all-start) | async-done | bytes 1048608 | tf_op jit(solution)/shard_map/all_to_all | solution.py:286
  23.0 29.8 %all_to_all.25 = bf16[8,2,4,128,128]{4,3,2,1,0:T(8,128)(2,1)} all-to-all(bf16[8,2,4,128,128]{4,3,2,1,0:T(8,128)(2,1)} %get-tuple-element.31), channel_id=1, replica_groups={{0,2,4,6,8,10,12,14},{16,18,20,22,24,26,28,30},{1,3,5,7,9,11,13,15},{17..., dimensions={0} | all-to-all | bytes 4194304 | tf_op jit(solution)/shard_map/all_to_all | solution.py:298
  52.7 3.6 %all-to-all-start.3 = ((bf16[8,2,4,128,128]{4,3,2,1,0:T(8,128)(2,1)}), bf16[8,2,4,128,128]{4,3,2,1,0:T(8,128)(2,1)S(1)}, u32[]{:S(2)}, u32[]{:S(2)}) async-start(bf16[8,2,4,128,128]{4,3,2,1,0:T(8,128)(2,1)} %get-tuple-element.40), calls=%async_computation.3 | async-start | bytes 4194304 | tf_op jit(solution)/shard_map/all_to_all | solution.py:298
  56.4 24.7 %all-to-all-done.3 = bf16[8,2,4,128,128]{4,3,2,1,0:T(8,128)(2,1)S(1)} async-done(((bf16[8,2,4,128,128]{4,3,2,1,0:T(8,128)(2,1)}), bf16[8,2,4,128,128]{4,3,2,1,0:T(8,128)(2,1)S(1)}, u32[]{:S(2)}, u32[]{:S(2)}) %all-to-all-start.3) | async-done | bytes 2097184 | tf_op jit(solution)/shard_map/all_to_all | solution.py:298
  81.1 1.0 fusion.14
  82.1 2.6 %collective-permute-start.1 = (bf16[8,128,256]{2,1,0:T(8,128)(2,1)S(1)}, bf16[8,128,256]{2,1,0:T(8,128)(2,1)S(1)}, u32[]{:S(2)}, u32[]{:S(2)}) collective-permute-start(bf16[8,128,256]{2,1,0:T(8,128)(2,1)S(1)} %get-tuple-element.50.q_ref), channel_id=1, source_target_pairs={{0,16},{2,18},{4,20},{6,22},{8,24},{10,26},{12,28},{14,30},{16,0},... | collective-permute-start | bytes 1572872 | tf_op jit(solution)/shard_map/ppermute | solution.py:294
  84.7 23.8 %collective-permute-done.1.q_ref = bf16[8,128,256]{2,1,0:T(8,128)(2,1)S(1)} collective-permute-done((bf16[8,128,256]{2,1,0:T(8,128)(2,1)S(1)}, bf16[8,128,256]{2,1,0:T(8,128)(2,1)S(1)}, u32[]{:S(2)}, u32[]{:S(2)}) %collective-permute-start.1) | collective-permute-done | bytes 524320 | tf_op jit(solution)/shard_map/ppermute | solution.py:294
  108.5 0.8 copy-done.6
  109.3 12.0 %attend.5 = (bf16[8,128,256]{2,1,0:T(8,128)(2,1)}, f32[8,8,128]{2,1,0:T(8,128)}) custom-call(s32[8,32]{1,0:T(8,128)} %bitcast.15, s32[8]{0:T(128)} %get-tuple-element.37.counts_ref, bf16[8,128,256]{2,1,0:T(8,128)(2,1)} %copy-done.6, bf16[16,4,128,128]{3,2,1,0:T(8,128)(2,1)} %bitcast.10, bf16[16,4,128,128]{3,2,1,0:T(8,128)(2,1)} %bitcast.5.far_ref), custom_call_target="tpu_custom_call" | custom-call | tf_op jit(solution)/shard_map/attend/pallas_call | solution.py:168
  121.4 2.9 %collective-permute-start.5 = (bf16[8,128,256]{2,1,0:T(8,128)(2,1)S(1)}, bf16[8,128,256]{2,1,0:T(8,128)(2,1)}, u32[]{:S(2)}, u32[]{:S(2)}) collective-permute-start(bf16[8,128,256]{2,1,0:T(8,128)(2,1)S(1)} %copy-done.2), channel_id=1, source_target_pairs={{0,16},{2,18},{4,20},{6,22},{8,24},{10,26},{12,28},{14,30},{16,0},... | collective-permute-start | bytes 1572872 | tf_op jit(solution)/shard_map/ppermute | solution.py:294
  124.4 16.8 %attend.4 = (bf16[8,128,256]{2,1,0:T(8,128)(2,1)}, f32[8,8,128]{2,1,0:T(8,128)}) custom-call(s32[8,32]{1,0:T(8,128)} %bitcast.13, s32[8]{0:T(128)} %get-tuple-element.26.counts_ref, bf16[8,128,256]{2,1,0:T(8,128)(2,1)} %copy-done.3, bf16[16,4,128,128]{3,2,1,0:T(8,128)(2,1)} %bitcast.11, bf16[16,4,128,128]{3,2,1,0:T(8,128)(2,1)} %bitcast.5.far_ref), custom_call_target="tpu_custom_call" | custom-call | tf_op jit(solution)/shard_map/attend/pallas_call | solution.py:168
  141.2 28.7 %collective-permute-done.3.sb_ref = f32[8,8,128]{2,1,0:T(8,128)S(1)} collective-permute-done((f32[8,8,128]{2,1,0:T(8,128)}, f32[8,8,128]{2,1,0:T(8,128)S(1)}, u32[]{:S(2)}, u32[]{:S(2)}) %collective-permute-start.3) | collective-permute-done | bytes 32800 | tf_op jit(solution)/shard_map/ppermute | solution.py:305
  170.7 2.9 %merge.2 = bf16[8,128,256]{2,1,0:T(8,128)(2,1)} custom-call(bf16[8,128,256]{2,1,0:T(8,128)(2,1)} %get-tuple-element.34.oa_ref, f32[8,8,128]{2,1,0:T(8,128)} %get-tuple-element.35.sa_ref, bf16[8,128,256]{2,1,0:T(8,128)(2,1)} %copy-done.4, f32[8,8,128]{2,1,0:T(8,128)} %copy-done.8), custom_call_target="tpu_custom_call" | custom-call | tf_op jit(solution)/shard_map/merge/pallas_call | solution.py:209
  173.6 3.5 %all-to-all-start.2 = ((bf16[8,128,256]{2,1,0:T(8,128)(2,1)}), bf16[8,128,256]{2,1,0:T(8,128)(2,1)S(1)}, u32[]{:S(2)}, u32[]{:S(2)}) async-start(bf16[8,128,256]{2,1,0:T(8,128)(2,1)} %merge.2), calls=%async_computation.2 | async-start | bytes 1048576 | tf_op jit(solution)/shard_map/all_to_all | solution.py:308
  177.1 11.9 %attend.7 = (bf16[8,128,256]{2,1,0:T(8,128)(2,1)}, f32[8,8,128]{2,1,0:T(8,128)}) custom-call(s32[8,32]{1,0:T(8,128)} %bitcast.16, s32[8]{0:T(128)} %get-tuple-element.37.counts_ref, bf16[8,128,256]{2,1,0:T(8,128)(2,1)} %collective-permute-done.5.q_ref, bf16[16,4,128,128]{3,2,1,0:T(8,128)(2,1)} %bitcast.8, bf16[16,4,128,128]{3,2,1,0:T(8,128)(2,1)} %bitcast.7.far_ref), custom_call_target="tpu_custom_call" | custom-call | tf_op jit(solution)/shard_map/attend/pallas_call | solution.py:168
  189.2 2.8 %collective-permute-start.7 = (f32[8,8,128]{2,1,0:T(8,128)}, f32[8,8,128]{2,1,0:T(8,128)S(1)}, u32[]{:S(2)}, u32[]{:S(2)}) collective-permute-start(f32[8,8,128]{2,1,0:T(8,128)} %get-tuple-element.44), channel_id=1, source_target_pairs={{0,16},{2,18},{4,20},{6,22},{8,24},{10,26},{12,28},{14,30},{16,0},... | collective-permute-start | bytes 98312 | tf_op jit(solution)/shard_map/ppermute | solution.py:305
  192.0 16.9 %attend.6 = (bf16[8,128,256]{2,1,0:T(8,128)(2,1)}, f32[8,8,128]{2,1,0:T(8,128)}) custom-call(s32[8,32]{1,0:T(8,128)} %bitcast.14, s32[8]{0:T(128)} %get-tuple-element.26.counts_ref, bf16[8,128,256]{2,1,0:T(8,128)(2,1)} %get-tuple-element.49.q_ref, bf16[16,4,128,128]{3,2,1,0:T(8,128)(2,1)} %bitcast.9, bf16[16,4,128,128]{3,2,1,0:T(8,128)(2,1)} %bitcast.7.far_ref), custom_call_target="tpu_custom_call" | custom-call | tf_op jit(solution)/shard_map/attend/pallas_call | solution.py:168
  208.9 5.6 %collective-permute-done.7.sb_ref = f32[8,8,128]{2,1,0:T(8,128)S(1)} collective-permute-done((f32[8,8,128]{2,1,0:T(8,128)}, f32[8,8,128]{2,1,0:T(8,128)S(1)}, u32[]{:S(2)}, u32[]{:S(2)}) %collective-permute-start.7) | collective-permute-done | bytes 32800 | tf_op jit(solution)/shard_map/ppermute | solution.py:305
  215.4 2.9 %merge.3 = bf16[8,128,256]{2,1,0:T(8,128)(2,1)} custom-call(bf16[8,128,256]{2,1,0:T(8,128)(2,1)} %get-tuple-element.41.oa_ref, f32[8,8,128]{2,1,0:T(8,128)} %get-tuple-element.42.sa_ref, bf16[8,128,256]{2,1,0:T(8,128)(2,1)} %copy-done.5, f32[8,8,128]{2,1,0:T(8,128)} %copy-done.7), custom_call_target="tpu_custom_call" | custom-call | tf_op jit(solution)/shard_map/merge/pallas_call | solution.py:209
  218.2 13.7 %all_to_all.26.refs_1_ = bf16[8,128,256]{2,1,0:T(8,128)(2,1)} all-to-all(bf16[8,128,256]{2,1,0:T(8,128)(2,1)} %merge.3), channel_id=1, replica_groups={{0,2,4,6,8,10,12,14},{16,18,20,22,24,26,28,30},{1,3,5,7,9,11,13,15},{17..., dimensions={0} | all-to-all | bytes 1048576 | tf_op jit(solution)/shard_map/all_to_all | solution.py:308
  231.9 2.3 join_columns.1
  (38 shorter events, 4.5 us)
Async XLA Ops:
  0.0 8.3 %copy-start.9 = (s32[32,32]{1,0:T(8,128)S(1)}, s32[32,32]{1,0:T(8,128)}, u32[]{:S(2)}) copy-start(s32[32,32]{1,0:T(8,128)} %param.7) | copy-start | bytes 12292
  2.1 20.9 %all-to-all-start = ((bf16[8,128,512]{2,1,0:T(8,128)(2,1)}), bf16[8,128,512]{2,1,0:T(8,128)(2,1)S(1)}, u32[]{:S(2)}, u32[]{:S(2)}) async-start(bf16[8,128,512]{2,1,0:T(8,128)(2,1)} %split_queries.1), calls=%async_computation | async-start | bytes 2097152 | tf_op jit(solution)/shard_map/all_to_all | solution.py:286
  52.7 28.4 %all-to-all-start.3 = ((bf16[8,2,4,128,128]{4,3,2,1,0:T(8,128)(2,1)}), bf16[8,2,4,128,128]{4,3,2,1,0:T(8,128)(2,1)S(1)}, u32[]{:S(2)}, u32[]{:S(2)}) async-start(bf16[8,2,4,128,128]{4,3,2,1,0:T(8,128)(2,1)} %get-tuple-element.40), calls=%async_computation.3 | async-start | bytes 4194304 | tf_op jit(solution)/shard_map/all_to_all | solution.py:298
  56.4 52.1 %collective-permute-start = (bf16[8,2,4,128,128]{4,3,2,1,0:T(8,128)(2,1)}, bf16[8,2,4,128,128]{4,3,2,1,0:T(8,128)(2,1)}, u32[]{:S(2)}, u32[]{:S(2)}) collective-permute-start(bf16[8,2,4,128,128]{4,3,2,1,0:T(8,128)(2,1)} %all_to_all.25), channel_id=1, source_target_pairs={{0,1},{1,0},{2,3},{3,2},{4,5},{5,4},{6,7},{7,6},{8,9},{9,8},{10,11... | collective-permute-start | bytes 6291464 | tf_op jit(solution)/shard_map/ppermute | solution.py:302
  81.1 40.2 %copy-start = (bf16[8,2,4,128,128]{4,3,2,1,0:T(8,128)(2,1)}, bf16[8,2,4,128,128]{4,3,2,1,0:T(8,128)(2,1)S(1)}, u32[]{:S(2)}) copy-start(bf16[8,2,4,128,128]{4,3,2,1,0:T(8,128)(2,1)S(1)} %all-to-all-done.3) | copy-start | bytes 6291460
  81.1 96.0 %collective-permute-start.4 = (bf16[8,2,4,128,128]{4,3,2,1,0:T(8,128)(2,1)S(1)}, bf16[8,2,4,128,128]{4,3,2,1,0:T(8,128)(2,1)}, u32[]{:S(2)}, u32[]{:S(2)}) collective-permute-start(bf16[8,2,4,128,128]{4,3,2,1,0:T(8,128)(2,1)S(1)} %all-to-all-done.3), channel_id=1, source_target_pairs={{0,1},{1,0},{2,3},{3,2},{4,5},{5,4},{6,7},{7,6},{8,9},{9,8},{10,11... | collective-permute-start | bytes 6291464 | tf_op jit(solution)/shard_map/ppermute | solution.py:302
  82.1 26.4 %copy-start.3 = (bf16[8,128,256]{2,1,0:T(8,128)(2,1)}, bf16[8,128,256]{2,1,0:T(8,128)(2,1)S(1)}, u32[]{:S(2)}) copy-start(bf16[8,128,256]{2,1,0:T(8,128)(2,1)S(1)} %get-tuple-element.50.q_ref) | copy-start | bytes 1572868
  82.1 26.4 %collective-permute-start.1 = (bf16[8,128,256]{2,1,0:T(8,128)(2,1)S(1)}, bf16[8,128,256]{2,1,0:T(8,128)(2,1)S(1)}, u32[]{:S(2)}, u32[]{:S(2)}) collective-permute-start(bf16[8,128,256]{2,1,0:T(8,128)(2,1)S(1)} %get-tuple-element.50.q_ref), channel_id=1, source_target_pairs={{0,16},{2,18},{4,20},{6,22},{8,24},{10,26},{12,28},{14,30},{16,0},... | collective-permute-start | bytes 1572872 | tf_op jit(solution)/shard_map/ppermute | solution.py:294
  108.5 0.8 copy-start.6
  109.3 12.1 %copy-start.2 = (bf16[8,128,256]{2,1,0:T(8,128)(2,1)S(1)}, bf16[8,128,256]{2,1,0:T(8,128)(2,1)}, u32[]{:S(2)}) copy-start(bf16[8,128,256]{2,1,0:T(8,128)(2,1)} %get-tuple-element.49.q_ref) | copy-start | bytes 1572868
  121.3 48.6 %collective-permute-start.2 = (bf16[8,128,256]{2,1,0:T(8,128)(2,1)}, bf16[8,128,256]{2,1,0:T(8,128)(2,1)S(1)}, u32[]{:S(2)}, u32[]{:S(2)}) collective-permute-start(bf16[8,128,256]{2,1,0:T(8,128)(2,1)} %get-tuple-element.38), channel_id=1, source_target_pairs={{0,16},{2,18},{4,20},{6,22},{8,24},{10,26},{12,28},{14,30},{16,0},... | collective-permute-start | bytes 1572872 | tf_op jit(solution)/shard_map/ppermute | solution.py:304
  121.4 55.7 %collective-permute-start.5 = (bf16[8,128,256]{2,1,0:T(8,128)(2,1)S(1)}, bf16[8,128,256]{2,1,0:T(8,128)(2,1)}, u32[]{:S(2)}, u32[]{:S(2)}) collective-permute-start(bf16[8,128,256]{2,1,0:T(8,128)(2,1)S(1)} %copy-done.2), channel_id=1, source_target_pairs={{0,16},{2,18},{4,20},{6,22},{8,24},{10,26},{12,28},{14,30},{16,0},... | collective-permute-start | bytes 1572872 | tf_op jit(solution)/shard_map/ppermute | solution.py:294
  124.3 45.6 %collective-permute-start.3 = (f32[8,8,128]{2,1,0:T(8,128)}, f32[8,8,128]{2,1,0:T(8,128)S(1)}, u32[]{:S(2)}, u32[]{:S(2)}) collective-permute-start(f32[8,8,128]{2,1,0:T(8,128)} %get-tuple-element.39), channel_id=1, source_target_pairs={{0,16},{2,18},{4,20},{6,22},{8,24},{10,26},{12,28},{14,30},{16,0},... | collective-permute-start | bytes 98312 | tf_op jit(solution)/shard_map/ppermute | solution.py:305
  169.9 0.6 copy-start.8
  169.9 0.8 copy-start.4
  173.6 44.6 %all-to-all-start.2 = ((bf16[8,128,256]{2,1,0:T(8,128)(2,1)}), bf16[8,128,256]{2,1,0:T(8,128)(2,1)S(1)}, u32[]{:S(2)}, u32[]{:S(2)}) async-start(bf16[8,128,256]{2,1,0:T(8,128)(2,1)} %merge.2), calls=%async_computation.2 | async-start | bytes 1048576 | tf_op jit(solution)/shard_map/all_to_all | solution.py:308
  189.0 25.5 %collective-permute-start.6 = (bf16[8,128,256]{2,1,0:T(8,128)(2,1)}, bf16[8,128,256]{2,1,0:T(8,128)(2,1)S(1)}, u32[]{:S(2)}, u32[]{:S(2)}) collective-permute-start(bf16[8,128,256]{2,1,0:T(8,128)(2,1)} %get-tuple-element.43), channel_id=1, source_target_pairs={{0,16},{2,18},{4,20},{6,22},{8,24},{10,26},{12,28},{14,30},{16,0},... | collective-permute-start | bytes 1572872 | tf_op jit(solution)/shard_map/ppermute | solution.py:304
  189.2 25.3 %collective-permute-start.7 = (f32[8,8,128]{2,1,0:T(8,128)}, f32[8,8,128]{2,1,0:T(8,128)S(1)}, u32[]{:S(2)}, u32[]{:S(2)}) collective-permute-start(f32[8,8,128]{2,1,0:T(8,128)} %get-tuple-element.44), channel_id=1, source_target_pairs={{0,16},{2,18},{4,20},{6,22},{8,24},{10,26},{12,28},{14,30},{16,0},... | collective-permute-start | bytes 98312 | tf_op jit(solution)/shard_map/ppermute | solution.py:305
  214.6 0.6 copy-start.7
  214.6 0.8 copy-start.5
  218.2 13.7 %copy-start.1 = (bf16[8,128,256]{2,1,0:T(8,128)(2,1)}, bf16[8,128,256]{2,1,0:T(8,128)(2,1)S(1)}, u32[]{:S(2)}) copy-start(bf16[8,128,256]{2,1,0:T(8,128)(2,1)S(1)} %all-to-all-done.2.refs_0_) | copy-start | bytes 1572868
